TPU v7x, 256 devices: a whole 4x4x8 slice. The times are simulated.
256 devices in a mesh: tm: 32 (over x, y, core), rows: 8 (over z).
Axes of the slice: x: 4, y: 4, z: 8, core: 2. Of those that a mesh axis runs over, the one named last changes fastest.
Arguments:
- latents: bfloat16 [64, 32, 64, 512], P('tm', 'rows'), may hold values from -128 to 128
- conv_weight: bfloat16 [27, 512, 512], P(None, 'tm'), may hold values from -0.0546875 to 0.0546875
- query_weight: bfloat16 [512, 512], replicated, may hold values from -1 to 4
- key_weight: bfloat16 [512, 512], replicated, may hold values from -1 to 4
- value_weight: bfloat16 [512, 512], replicated, may hold values from -0.25 to 0.25
- out_weight: bfloat16 [512, 512], replicated, may hold values from -1.5 to 1.5
Outputs:
- output: bfloat16 [64, 32, 64, 512], P('tm', 'rows')
All inputs are finite; a program needn't handle non-finite values.
Results may differ from a plain program's by a relative error of at most 0.028.
Values may be sent and summed in bfloat16 or wider, within the bound.
A program may use at most 128 MiB of HBM per device.

v0:
```python
import jax
import jax.numpy as jnp
from jax import lax
from jax.sharding import PartitionSpec as P

G = 32


epsilon = 1e-06


def with_halo(block, sides, width):
    for axis, dim in sides:
        count = lax.axis_size(axis)
        forward = [(i, i + 1) for i in range(count - 1)]
        backward = [(target, source) for source, target in forward]
        low = lax.ppermute(
            lax.slice_in_dim(block, block.shape[dim] - width, None, axis=dim), axis, forward
        )
        high = lax.ppermute(lax.slice_in_dim(block, 0, width, axis=dim), axis, backward)
        block = jnp.concatenate([low, block, high], axis=dim)
    return block


def from_behind(shard, axis, by):
    devices = lax.axis_size(axis)
    pairs = [(i, i + by) for i in range(devices) if 0 <= i + by < devices]
    return lax.ppermute(shard, axis, pairs)


def body(latents, conv_weight, query_weight, key_weight, value_weight, out_weight):
    frames, rows_here, columns, chans = latents.shape
    framed = with_halo(latents, (("rows", 1),), 1)
    earlier = from_behind(framed, "tm", 1)
    window = jnp.concatenate([earlier, framed], axis=0)
    window = jnp.pad(window, ((0, 0), (0, 0), (1, 1), (0, 0)))
    tokens_here = frames * rows_here * columns
    initial = jnp.zeros((tokens_here, chans), jnp.float32)
    totals = initial
    kernel_piece = lax.all_gather(conv_weight, "tm", axis=1, tiled=True)
    channels_in = kernel_piece.shape[1]
    for tap_index in range(27):
        frame_lag = tap_index // 9
        row_lag = tap_index // 3 % 3
        col_lag = tap_index % 3
        patches = window[
            frame_lag : frame_lag + frames,
            row_lag : row_lag + rows_here,
            col_lag : col_lag + columns,
            :,
        ]
        patches = patches.reshape(tokens_here, channels_in)
        totals = totals + jnp.dot(
            patches, kernel_piece[tap_index], preferred_element_type=jnp.float32
        )
    convolved = totals.astype(jnp.bfloat16)
    per_frame = rows_here * columns
    entries = rows_here * lax.axis_size("rows") * columns * (chans // G)
    grouped = convolved.astype(jnp.float32).reshape(frames, per_frame, G, chans // G)
    group_total = lax.psum(jnp.sum(grouped, axis=(1, 3)), "rows")
    average = group_total / entries
    centered = grouped - average[:, None, :, None]
    spread = lax.psum(jnp.sum(centered * centered, axis=(1, 3)), "rows")
    variance = spread / entries
    normed = (
        (centered * lax.rsqrt(variance + epsilon)[:, None, :, None])
        .reshape(tokens_here, chans)
        .astype(jnp.bfloat16)
    )
    queries = (
        jnp.dot(normed, query_weight, preferred_element_type=jnp.float32)
        .astype(jnp.bfloat16)
        .reshape(frames, per_frame, chans)
    )
    keys = (
        jnp.dot(normed, key_weight, preferred_element_type=jnp.float32)
        .astype(jnp.bfloat16)
        .reshape(frames, per_frame, chans)
    )
    values = (
        jnp.dot(normed, value_weight, preferred_element_type=jnp.float32)
        .astype(jnp.bfloat16)
        .reshape(frames, per_frame, chans)
    )
    score_scale = chans ** (-0.5)
    all_keys, all_values = (
        lax.all_gather(keys, "rows", axis=1, tiled=True),
        lax.all_gather(values, "rows", axis=1, tiled=True),
    )
    scores = (
        jnp.einsum("fqc,fkc->fqk", queries, all_keys, preferred_element_type=jnp.float32)
        * score_scale
    )
    row_max = jnp.max(scores, axis=2)
    exp_weights = jnp.exp(scores - row_max[:, :, None]).astype(jnp.bfloat16)
    denominator = jnp.sum(exp_weights.astype(jnp.float32), axis=2)
    numerator = jnp.einsum(
        "fqk,fkc->fqc", exp_weights, all_values, preferred_element_type=jnp.float32
    )
    attended = (
        (numerator / denominator[:, :, None]).astype(jnp.bfloat16).reshape(tokens_here, chans)
    )
    summed = convolved.astype(jnp.float32) + jnp.dot(
        attended, out_weight, preferred_element_type=jnp.float32
    )
    return summed.astype(jnp.bfloat16).reshape(frames, rows_here, columns, chans)


def solution(mesh):
    placed = (P("tm", "rows", None, None), P(None, "tm", None), P(), P(), P(), P())
    return jax.shard_map(
        body, mesh=mesh, in_specs=placed, out_specs=P("tm", "rows", None, None), check_vma=False
    )
```

profile of v0, /device:TPU:1, one launch (start us, length us, event | category | flops | bytes accessed | tf_op | source)
XLA Modules:
  0.0 302.5 jit_solution(5250531530371219572)
XLA Ops:
  8.3 4.4 %collective-permute-start = (bf16[2,1,64,512]{3,2,1,0:T(8,128)(2,1)S(1)}, bf16[2,1,64,512]{3,2,1,0:T(8,128)(2,1)S(1)}, u32[]{:S(2)}, u32[]{:S(2)}) collective-permute-start(bf16[2,1,64,512]{3,2,1,0:T(8,128)(2,1)S(1)} %get-tuple-element.33), channel_id=1, source_target_pairs={{0,1},{1,2},{2,3},{3,4},{4,5},{5,6},{6,7},{8,9},{9,10},{10,11},{11... | collective-permute-start | bytes 393224 | tf_op jit(solution)/shard_map/ppermute | solution.py:17
  12.7 1.3 collective-permute-start.1
  14.8 4.2 %collective-permute-done.1 = bf16[2,1,64,512]{3,2,1,0:T(8,128)(2,1)S(1)} collective-permute-done((bf16[2,1,64,512]{3,2,1,0:T(8,128)(2,1)S(1)}, bf16[2,1,64,512]{3,2,1,0:T(8,128)(2,1)S(1)}, u32[]{:S(2)}, u32[]{:S(2)}) %collective-permute-start.1) | collective-permute-done | bytes 131104 | tf_op jit(solution)/shard_map/ppermute | solution.py:20
  19.0 2.6 pad_maximum_fusion.1
  21.6 4.7 %collective-permute-start.2 = (bf16[2,6,64,512]{3,2,1,0:T(8,128)(2,1)S(1)}, bf16[2,6,64,512]{3,2,1,0:T(8,128)(2,1)S(1)}, u32[]{:S(2)}, u32[]{:S(2)}) collective-permute-start(bf16[2,6,64,512]{3,2,1,0:T(8,128)(2,1)S(1)} %constant_dynamic-update-slice_fusion), channel_id=1, source_target_pairs={{0,8},{8,16},{16,24},{24,32},{32,40},{40,48},{48,56},{56,64},{64,7... | collective-permute-start | bytes 2359304 | tf_op jit(solution)/shard_map/ppermute | solution.py:28
  26.3 16.0 %collective-permute-done.2 = bf16[2,6,64,512]{3,2,1,0:T(8,128)(2,1)S(1)} collective-permute-done((bf16[2,6,64,512]{3,2,1,0:T(8,128)(2,1)S(1)}, bf16[2,6,64,512]{3,2,1,0:T(8,128)(2,1)S(1)}, u32[]{:S(2)}, u32[]{:S(2)}) %collective-permute-start.2) | collective-permute-done | bytes 786464 | tf_op jit(solution)/shard_map/ppermute | solution.py:28
  42.5 2.4 pad_slice_fusion.8
  44.9 2.8 pad_slice_fusion.7
  47.7 1.8 fusion.13
  49.5 40.0 %all-gather.4.cloned.1.call-done = bf16[27,512,512]{2,1,0:T(8,128)(2,1)} async-done(((bf16[27,16,512]{2,1,0:T(8,128)(2,1)}), bf16[27,512,512]{2,1,0:T(8,128)(2,1)}) %all-gather.4.cloned.1.call-update) | async-done | bytes 14155792 | tf_op jit(solution)/shard_map/all_gather | solution.py:40
  89.5 1.8 fusion.22
  91.3 2.0 fusion.21
  93.3 2.2 fusion.20
  95.5 1.7 fusion.19
  97.2 1.7 fusion.18
  98.9 1.7 fusion.17
  100.6 1.6 fusion.16
  112.1 1.3 copy.7
  113.5 1.9 reshape.133
  115.7 23.1 %psum.14 = f32[2,32]{0,1:T(8,128)S(1)} all-reduce(f32[2,32]{0,1:T(8,128)S(1)} %reduce_sum.27), channel_id=1, replica_groups=mesh['tm'=32,'rows'=8] {'rows'}, use_global_device_ids=true, to_apply=%region_1.2 | all-reduce | flops 64 | bytes 512 | tf_op jit(solution)/shard_map/psum | solution.py:60
  139.6 20.3 %psum.15 = f32[2,32]{0,1:T(8,128)S(1)} all-reduce(f32[2,32]{0,1:T(8,128)S(1)} %multiply_reduce_fusion.1), channel_id=1, replica_groups=mesh['tm'=32,'rows'=8] {'rows'}, use_global_device_ids=true, to_apply=%region_3.4 | all-reduce | flops 64 | bytes 512 | tf_op jit(solution)/shard_map/psum | solution.py:63
  161.3 1.6 copy.9
  164.2 2.5 copy.8
  166.8 1.5 multiply_convert_fusion
  168.3 1.3 convolution_convert_fusion.1
  169.7 2.3 convolution_convert_fusion
  172.4 62.3 %all-gather.6.cloned.1.call-done = bf16[2,2048,512]{2,1,0:T(8,128)(2,1)} async-done(((bf16[2,256,512]{2,1,0:T(8,128)(2,1)}), bf16[2,2048,512]{2,1,0:T(8,128)(2,1)}) %all-gather.6.cloned.1.call-update) | async-done | bytes 4194320 | tf_op jit(solution)/shard_map/all_gather | solution.py:87
  234.8 3.6 %multiply_reduce_fusion = (f32[2,256]{1,0:T(2,128)S(1)}, f32[2,256,2048]{2,1,0:T(8,128)S(1)}) fusion(bf16[2,256,512]{2,1,0:T(8,128)(2,1)S(1)} %bitcast.168, bf16[2,2048,512]{2,1,0:T(8,128)(2,1)} %all-gather.6.cloned.1.call-done), kind=kOutput, calls=%fused_computation.2 | convolution fusion | flops 1075838464 | bytes 8914944 | tf_op jit(solution)/shard_map/fqc,fkc->fqk/dot_general | solution.py:91
  238.3 2.0 copy-done.1
  241.1 48.8 %all-gather.8.cloned.1.call-done = bf16[2,2048,512]{2,1,0:T(8,128)(2,1)} async-done(((bf16[2,256,512]{2,1,0:T(8,128)(2,1)}), bf16[2,2048,512]{2,1,0:T(8,128)(2,1)}) %all-gather.8.cloned.1.call-update) | async-done | bytes 4194320 | tf_op jit(solution)/shard_map/all_gather | solution.py:88
  289.9 4.8 %fusion.10 = bf16[2,256,512]{2,1,0:T(8,128)(2,1)S(1)} fusion(bf16[2,2048,512]{2,1,0:T(8,128)(2,1)} %all-gather.8.cloned.1.call-done, f32[2,256]{1,0:T(2,128)S(1)} %convert_reduce_fusion, f32[2,256,2048]{2,1,0:T(8,128)} %copy-done.1, f32[2,256]{1,0:T(2,128)S(1)} %get-tuple-element.34), kind=kOutput, calls=%fused_computation.43 | convolution fusion | flops 1077411840 | bytes 8916992 | tf_op jit(solution)/shard_map/fqk,fkc->fqc/dot_general | solution.py:97
  294.7 1.2 fusion.9
  (84 shorter events, 17.6 us)
Async XLA Ops:
  6.5 161.7 %copy-start = (bf16[512,512]{1,0:T(8,128)(2,1)S(1)}, bf16[512,512]{1,0:T(8,128)(2,1)}, u32[]{:S(2)}) copy-start(bf16[512,512]{1,0:T(8,128)(2,1)} %param.9) | copy-start | bytes 1572868
  6.5 83.0 %all-gather.4.cloned.1.call-start = ((), (), s32[]{:S(2)}) async-start(), calls=%async_computation | async-start | bytes 14598144 | tf_op jit(solution)/shard_map/all_gather | solution.py:40
  7.3 227.5 %all-gather.6.cloned.1.call-start = ((), (), s32[]{:S(2)}) async-start(), calls=%async_computation.1 | async-start | bytes 4718592 | tf_op jit(solution)/shard_map/all_gather | solution.py:87
  8.3 6.5 %collective-permute-start = (bf16[2,1,64,512]{3,2,1,0:T(8,128)(2,1)S(1)}, bf16[2,1,64,512]{3,2,1,0:T(8,128)(2,1)S(1)}, u32[]{:S(2)}, u32[]{:S(2)}) collective-permute-start(bf16[2,1,64,512]{3,2,1,0:T(8,128)(2,1)S(1)} %get-tuple-element.33), channel_id=1, source_target_pairs={{0,1},{1,2},{2,3},{3,4},{4,5},{5,6},{6,7},{8,9},{9,10},{10,11},{11... | collective-permute-start | bytes 393224 | tf_op jit(solution)/shard_map/ppermute | solution.py:17
  12.7 6.4 %collective-permute-start.1 = (bf16[2,1,64,512]{3,2,1,0:T(8,128)(2,1)S(1)}, bf16[2,1,64,512]{3,2,1,0:T(8,128)(2,1)S(1)}, u32[]{:S(2)}, u32[]{:S(2)}) collective-permute-start(bf16[2,1,64,512]{3,2,1,0:T(8,128)(2,1)S(1)} %get-tuple-element.32), channel_id=1, source_target_pairs={{1,0},{2,1},{3,2},{4,3},{5,4},{6,5},{7,6},{9,8},{10,9},{11,10},{12... | collective-permute-start | bytes 393224 | tf_op jit(solution)/shard_map/ppermute | solution.py:20
  21.6 20.8 %collective-permute-start.2 = (bf16[2,6,64,512]{3,2,1,0:T(8,128)(2,1)S(1)}, bf16[2,6,64,512]{3,2,1,0:T(8,128)(2,1)S(1)}, u32[]{:S(2)}, u32[]{:S(2)}) collective-permute-start(bf16[2,6,64,512]{3,2,1,0:T(8,128)(2,1)S(1)} %constant_dynamic-update-slice_fusion), channel_id=1, source_target_pairs={{0,8},{8,16},{16,24},{24,32},{32,40},{40,48},{48,56},{56,64},{64,7... | collective-permute-start | bytes 2359304 | tf_op jit(solution)/shard_map/ppermute | solution.py:28
  89.5 12.7 %copy-start.2 = (bf16[27,512,512]{2,1,0:T(8,128)(2,1)S(1)}, bf16[27,512,512]{2,1,0:T(8,128)(2,1)}, u32[]{:S(2)}) copy-start(bf16[27,512,512]{2,1,0:T(8,128)(2,1)} %all-gather.4.cloned.1.call-done) | copy-start | bytes 42467332
  95.5 6.8 %copy-start.10 = (bf16[2,4,64,512]{3,2,1,0:T(8,128)(2,1)S(1)}, bf16[2,4,64,512]{3,2,1,0:T(8,128)(2,1)}, u32[]{:S(2)}) copy-start(bf16[2,4,64,512]{3,2,1,0:T(8,128)(2,1)} %get-tuple-element.19) | copy-start | bytes 1572868
  97.2 5.5 %copy-start.9 = (bf16[2,4,64,512]{3,2,1,0:T(8,128)(2,1)S(1)}, bf16[2,4,64,512]{3,2,1,0:T(8,128)(2,1)}, u32[]{:S(2)}) copy-start(bf16[2,4,64,512]{3,2,1,0:T(8,128)(2,1)} %get-tuple-element.21) | copy-start | bytes 1572868
  98.9 4.3 %copy-start.16 = (bf16[2,4,64,512]{3,2,1,0:T(8,128)(2,1)S(1)}, bf16[2,4,64,512]{3,2,1,0:T(8,128)(2,1)}, u32[]{:S(2)}) copy-start(bf16[2,4,64,512]{3,2,1,0:T(8,128)(2,1)} %get-tuple-element.6) | copy-start | bytes 1572868
  102.3 1.4 copy-start.11
  103.2 1.1 copy-start.17
  103.6 1.1 copy-start.8
  104.1 1.1 copy-start.15
  104.7 1.1 copy-start.7
  105.2 1.1 copy-start.14
  105.7 1.1 copy-start.6
  106.2 1.1 copy-start.13
  106.7 1.1 copy-start.5
  107.2 1.1 copy-start.12
  107.8 1.1 copy-start.4
  108.3 1.1 copy-start.19
  109.3 1.1 copy-start.3
  110.4 1.3 copy-start.18
  168.3 3.7 %copy-start.20 = (bf16[512,512]{1,0:T(8,128)(2,1)S(1)}, bf16[512,512]{1,0:T(8,128)(2,1)}, u32[]{:S(2)}) copy-start(bf16[512,512]{1,0:T(8,128)(2,1)} %param.8) | copy-start | bytes 1572868
  169.6 120.3 %all-gather.8.cloned.1.call-start = ((), (), s32[]{:S(2)}) async-start(), calls=%async_computation.2 | async-start | bytes 4718592 | tf_op jit(solution)/shard_map/all_gather | solution.py:88
  238.3 2.0 copy-start.1
  241.1 53.6 %copy-start.21 = (bf16[512,512]{1,0:T(8,128)(2,1)S(1)}, bf16[512,512]{1,0:T(8,128)(2,1)}, u32[]{:S(2)}) copy-start(bf16[512,512]{1,0:T(8,128)(2,1)} %param.11) | copy-start | bytes 1572868
Sparse Core Ops, SparseCore 0:
  10.0 79.4 all-gather.3
  169.7 64.9 all-gather.5
  236.6 53.3 all-gather.7
where the time goes:
time: 303 us
  waiting for transfers between devices  173 us (57%)
  blocking collectives  43.4 us (14%)
  matrix products  34.9 us (12%)
  local copies, waits for them, and re-layouts  19.3 us (6%)
  between operations  13.6 us (4%)
  starting transfers between devices  10.5 us (3%)
  other arithmetic  7.89 us (3%)
    all_gather x1, waiting for transfers between devices, body(): lax.all_gather(keys, 'rows', axis=1, tiled=True)  62.3 us
    all_gather x1, waiting for transfers between devices, body(): lax.all_gather(values, 'rows', axis=1, tiled=True)  48.8 us
    all_gather x1, waiting for transfers between devices, body(): kernel_piece = lax.all_gather(conv_weight, 'tm', axis=1, tiled=True)  40 us
    psum x1, blocking collectives, body(): group_total = lax.psum(jnp.sum(grouped, axis=(1, 3)), 'rows')  23.1 us
    dot_general x27, matrix products, body(): jnp.dot(patches, kernel_piece[tap_index], preferred_element_type=jnp.floa...  21.4 us
    psum x1, blocking collectives, body(): spread = lax.psum(jnp.sum(centered * centered, axis=(1, 3)), 'rows')  20.3 us
    ppermute x1, waiting for transfers between devices, from_behind(): return lax.ppermute(shard, axis, pairs)  16 us
  transfers between devices with their start and end apart: 6, of which 6 were waited for; matrix products, arithmetic and copies ran while one was open for 6% of the time, Pallas kernels for 0%

commit v1 on v0

v1 whole, which is shorter than its diff:
```python
import functools

import jax
import jax.numpy as jnp
from jax import lax
from jax.experimental import pallas as pl
from jax.experimental.pallas import tpu as pltpu
from jax.sharding import PartitionSpec as P

MESH = pl.DeviceIdType.MESH
F32 = jnp.float32
BF16 = jnp.bfloat16

GROUPS = 32
EPSILON = 1e-06
LOG2E = 1.4426950408889634
NX, NY, NC, NZ = 4, 4, 2, 8
TAPS = 27
CHUNKS = 4

A, A1, A2 = (0, 14), (0, 7), (7, 7)
B, B1, B2 = (14, 13), (14, 7), (21, 6)


def kernel(
    lat, cw, wq, wk, wv, wo, out,
    raw, win, w, kv, acc, st, wts, qq, qb, mx, den, num,
    w_send, w_recv, d_send, d_recv, z_send, z_recv, h_send, h_recv, s_send, s_recv, loc,
):
    tm = lax.axis_index("tm")
    z = lax.axis_index("rows")
    x, y, core = tm // (NY * NC), tm // NC % NY, tm % NC
    mate = tm + 1 - 2 * core
    ntm = NX * NY * NC

    def at(px, py):
        return (px * NY + py) * NC + core

    def xs(d):
        return (x + d + NX) % NX

    def ys(d):
        return (y + d + NY) % NY

    def zs(d):
        return (z + d + NZ) % NZ

    def copy(src, dst, ss, rs, to_tm, to_z):
        return pltpu.make_async_remote_copy(
            src_ref=src, dst_ref=dst, send_sem=ss, recv_sem=rs,
            device_id={"tm": to_tm, "rows": to_z}, device_id_type=MESH,
        )

    sent = []

    def send(src, dst, ss, rs, to_tm, to_z):
        c = copy(src, dst, ss, rs, to_tm, to_z)
        c.start()
        sent.append((src, ss))

    def arrived(ref, rs):
        copy(ref, ref, rs, rs, mate, z).wait_recv()

    barrier = pltpu.get_barrier_semaphore()
    peers = [(at(xs(1), y), z), (at(xs(-1), y), z), (at(x, ys(1)), z), (at(x, ys(-1)), z)]
    peers += [(mate, z), ((tm + 1) % ntm, z), ((tm + ntm - 1) % ntm, z)]
    peers += [(tm, zs(d)) for d in range(1, NZ)]
    for ptm, pz in peers:
        pl.semaphore_signal(barrier, inc=1, device_id={"tm": ptm, "rows": pz}, device_id_type=MESH)
    pl.semaphore_wait(barrier, len(peers))

    chans = lat.shape[3]
    cols = chans // CHUNKS

    def own(j, part):
        return cw.at[part[0] : part[0] + part[1], :, j * cols : (j + 1) * cols]

    def piece(j, px, py, part):
        return w.at[j, px, py, core, part[0] : part[0] + part[1]]

    def line_x(j, py, part):
        return w.at[j, :, py, core, part[0] : part[0] + part[1]]

    def line_y(j, px, part):
        return w.at[j, px, :, core, part[0] : part[0] + part[1]]

    def sems(j, r):
        return [(w_send.at[j, r, i], w_recv.at[j, r, i]) for i in range(4)]

    def start_1a(j):
        s = sems(j, 0)
        send(own(j, A), piece(j, x, y, A), *s[0], at(xs(1), y), z)
        send(own(j, B), piece(j, x, y, B), *s[2], at(x, ys(1)), z)
        send(own(j, A), piece(j, x, y, A), *s[1], at(xs(-1), y), z)
        send(own(j, B), piece(j, x, y, B), *s[3], at(x, ys(-1)), z)

    def start_1b(j):
        r = w_recv
        arrived(piece(j, xs(-1), y, A), r.at[j, 0, 0])
        s = sems(j, 1)
        src = piece(j, xs(-1), y, A1)
        send(src, src, *s[0], at(xs(1), y), z)
        arrived(piece(j, x, ys(-1), B), r.at[j, 0, 2])
        src = piece(j, x, ys(-1), B1)
        send(src, src, *s[2], at(x, ys(1)), z)
        arrived(piece(j, xs(1), y, A), r.at[j, 0, 1])
        src = piece(j, xs(1), y, A2)
        send(src, src, *s[1], at(xs(-1), y), z)
        arrived(piece(j, x, ys(1), B), r.at[j, 0, 3])
        src = piece(j, x, ys(1), B2)
        send(src, src, *s[3], at(x, ys(-1)), z)

    def to_mate(j, i, ref):
        send(ref, ref, d_send.at[j, i], d_recv.at[j, i], mate, z)

    def start_2a(j):
        r = w_recv
        arrived(piece(j, xs(2), y, A1), r.at[j, 1, 0])
        arrived(piece(j, xs(2), y, A2), r.at[j, 1, 1])
        arrived(piece(j, x, ys(2), B1), r.at[j, 1, 2])
        arrived(piece(j, x, ys(2), B2), r.at[j, 1, 3])
        pltpu.make_async_copy(
            cw.at[:, :, j * cols : (j + 1) * cols], w.at[j, x, y, core], loc.at[j]
        ).wait()
        s = sems(j, 2)
        la, lb = line_x(j, y, A), line_y(j, x, B)
        send(la, la, *s[0], at(x, ys(1)), z)
        send(lb, lb, *s[2], at(xs(1), y), z)
        send(la, la, *s[1], at(x, ys(-1)), z)
        send(lb, lb, *s[3], at(xs(-1), y), z)
        to_mate(j, 0, la)
        to_mate(j, 1, lb)

    def start_2b(j):
        r = w_recv
        s = sems(j, 3)
        arrived(line_x(j, ys(-1), A), r.at[j, 2, 0])
        src = line_x(j, ys(-1), A1)
        send(src, src, *s[0], at(x, ys(1)), z)
        arrived(line_y(j, xs(-1), B), r.at[j, 2, 2])
        src = line_y(j, xs(-1), B1)
        send(src, src, *s[2], at(xs(1), y), z)
        arrived(line_x(j, ys(1), A), r.at[j, 2, 1])
        src = line_x(j, ys(1), A2)
        send(src, src, *s[1], at(x, ys(-1)), z)
        arrived(line_y(j, xs(1), B), r.at[j, 2, 3])
        src = line_y(j, xs(1), B2)
        send(src, src, *s[3], at(xs(-1), y), z)
        to_mate(j, 2, line_x(j, ys(-1), A))
        to_mate(j, 3, line_y(j, xs(-1), B))
        to_mate(j, 4, line_x(j, ys(1), A))
        to_mate(j, 5, line_y(j, xs(1), B))

    def finish_gather(j):
        r = w_recv
        arrived(line_x(j, ys(2), A1), r.at[j, 3, 0])
        arrived(line_x(j, ys(2), A2), r.at[j, 3, 1])
        to_mate(j, 6, line_x(j, ys(2), A))
        arrived(line_y(j, xs(2), B1), r.at[j, 3, 2])
        arrived(line_y(j, xs(2), B2), r.at[j, 3, 3])
        to_mate(j, 7, line_y(j, xs(2), B))
        other = 1 - core
        for i, (d, whole) in enumerate(
            ((0, True), (0, False), (-1, True), (-1, False), (1, True), (1, False), (2, True), (2, False))
        ):
            if whole:
                ref = w.at[j, :, ys(d), other, A[0] : A[0] + A[1]]
            else:
                ref = w.at[j, xs(d), :, other, B[0] : B[0] + B[1]]
            arrived(ref, d_recv.at[j, i])

    def z_send_pair(j, r, up, down):
        send(up, up, z_send.at[j, r, 0], z_recv.at[j, r, 0], tm, zs(1))
        send(down, down, z_send.at[j, r, 1], z_recv.at[j, r, 1], tm, zs(-1))

    def z_step(j, r):
        if r == 0:
            z_send_pair(j, 0, kv.at[j, z], kv.at[j, z])
            return
        if r < 4:
            from_low, from_high = kv.at[j, zs(-r)], kv.at[j, zs(r)]
        else:
            from_low, from_high = kv.at[j, zs(4), 0], kv.at[j, zs(4), 1]
        arrived(from_low, z_recv.at[j, r - 1, 0])
        arrived(from_high, z_recv.at[j, r - 1, 1])
        if r < 3:
            z_send_pair(j, r, from_low, from_high)
        elif r == 3:
            z_send_pair(j, 3, kv.at[j, zs(-3), 0], kv.at[j, zs(3), 1])

    start_1a(0)
    locals_ = [pltpu.make_async_copy(lat, raw.at[2:4, 1:5], loc.at[CHUNKS])]
    for j in range(CHUNKS):
        locals_.append(
            pltpu.make_async_copy(cw.at[:, :, j * cols : (j + 1) * cols], w.at[j, x, y, core], loc.at[j])
        )
    for i, m in enumerate((wq, wk, wv, wo)):
        locals_.append(pltpu.make_async_copy(m, wts.at[i], loc.at[CHUNKS + 1 + i]))
    nxt = (tm + 1) % ntm
    send(lat.at[:, 0], raw.at[0:2, 1], h_send.at[0], h_recv.at[0], nxt, z)
    send(lat.at[:, 3], raw.at[0:2, 4], h_send.at[1], h_recv.at[1], nxt, z)
    send(lat.at[:, 1:3], raw.at[0:2, 2:4], h_send.at[2], h_recv.at[2], nxt, z)
    send(lat.at[:, 0], raw.at[2:4, 5], h_send.at[3], h_recv.at[3], tm, zs(-1))
    send(lat.at[:, 3], raw.at[2:4, 0], h_send.at[4], h_recv.at[4], tm, zs(1))
    for c in locals_:
        c.start()

    start_1b(0)
    start_2a(0)
    start_1a(1)
    arrived(raw.at[0:2, 1], h_recv.at[0])
    send(raw.at[0:2, 1], raw.at[0:2, 5], h_send.at[5], h_recv.at[5], tm, zs(-1))
    arrived(raw.at[0:2, 4], h_recv.at[1])
    send(raw.at[0:2, 4], raw.at[0:2, 0], h_send.at[6], h_recv.at[6], tm, zs(1))
    start_1b(1)
    start_2b(0)
    start_2a(1)
    start_1a(2)
    arrived(raw.at[0:2, 2:4], h_recv.at[2])
    arrived(raw.at[2:4, 5], h_recv.at[3])
    arrived(raw.at[2:4, 0], h_recv.at[4])
    arrived(raw.at[0:2, 5], h_recv.at[5])
    arrived(raw.at[0:2, 0], h_recv.at[6])
    locals_[0].wait()

    col = lax.broadcasted_iota(jnp.int32, (lat.shape[2], chans), 0)

    def shift(i, carry):
        f, r = i // 6, i % 6
        outside = ((r == 0) & (z == 0)) | ((r == 5) & (z == NZ - 1)) | ((f < 2) & (tm == 0))
        keep = jnp.where(outside, 0.0, 1.0).astype(F32)
        v = raw[f, r].astype(F32) * keep
        win[1, f, r] = v.astype(BF16)
        last = lat.shape[2] - 1
        win[0, f, r] = jnp.where(col == 0, 0.0, pltpu.roll(v, 1, 0)).astype(BF16)
        win[2, f, r] = jnp.where(col == last, 0.0, pltpu.roll(v, last, 0)).astype(BF16)
        return carry

    lax.fori_loop(0, 24, shift, 0)

    tokens = 2 * 4 * lat.shape[2]
    per_frame = tokens // 2

    def conv(j, lo, hi):
        def step(i, carry):
            dt, dr = i // 3, i % 3
            total = None
            for dc in range(3):
                patch = win[dc, pl.ds(dt, 2), pl.ds(dr, 4)].reshape(tokens, chans)
                tap = w[j, :, :, :, i * 3 + dc].reshape(chans, cols)
                term = jnp.dot(patch, tap, preferred_element_type=F32)
                total = term if total is None else total + term
            acc[...] += total
            return carry

        lax.fori_loop(lo, hi, step, 0)

    lane = lax.broadcasted_iota(jnp.int32, (cols, cols), 0)
    lane2 = lax.broadcasted_iota(jnp.int32, (cols, cols), 1)
    width = chans // GROUPS
    same = (lane // width == lane2 // width).astype(F32)
    count = per_frame * width

    def group_sum(v):
        return jnp.dot(v, same, preferred_element_type=F32, precision=lax.Precision.HIGHEST)

    def finish_chunk(j):
        c = acc[...].astype(BF16).reshape(2, per_frame, cols)
        kv[j, z] = c
        cf = c.astype(F32)
        mean = group_sum(jnp.sum(cf, axis=1)) * (1.0 / count)
        dev = cf - mean[:, None, :]
        st[z, 0:2, j * cols : (j + 1) * cols] = mean
        st[z, 2:4, j * cols : (j + 1) * cols] = group_sum(jnp.sum(dev * dev, axis=1))
        z_step(j, 0)

    for j in range(CHUNKS):
        finish_gather(j)
        if j >= 1:
            z_step(j - 1, 1)
        acc[...] = jnp.zeros_like(acc)
        conv(j, 0, 3)
        if j + 1 < CHUNKS:
            if j >= 1:
                pass
            start_2b(j + 1)
        if j >= 1:
            z_step(j - 1, 2)
        if j + 2 < CHUNKS:
            start_1b(j + 2)
        conv(j, 3, 6)
        if j + 2 < CHUNKS:
            start_2a(j + 2)
        if j + 3 < CHUNKS:
            start_1a(j + 3)
        if j >= 1:
            z_step(j - 1, 3)
        conv(j, 6, 9)
        finish_chunk(j)
        if j >= 1:
            z_step(j - 1, 4)

    last = CHUNKS - 1
    for d in range(1, NZ):
        send(st.at[z], st.at[z], s_send.at[d - 1], s_recv.at[d - 1], tm, zs(d))
    z_step(last, 1)
    for d in range(1, NZ):
        arrived(st.at[zs(-d)], s_recv.at[d - 1])
    for c in locals_[1 + CHUNKS :]:
        c.wait()

    means = st[:, 0:2, :]
    mean = jnp.sum(means, axis=0) * (1.0 / NZ)
    apart = means - mean[None]
    spread = jnp.sum(st[:, 2:4, :], axis=0) + count * jnp.sum(apart * apart, axis=0)
    rstd = lax.rsqrt(spread * (1.0 / (count * NZ)) + EPSILON)

    def whole(zb, f):
        return jnp.concatenate([kv[j, zb, f] for j in range(CHUNKS)], axis=1)

    for f in range(2):
        mf, rf = mean[f : f + 1], rstd[f : f + 1]
        n = ((whole(z, f).astype(F32) - mf) * rf).astype(BF16)
        q = jnp.dot(n, wts[0], preferred_element_type=F32).astype(BF16)
        qk = lax.dot_general(q, wts[1], (((1,), (1,)), ((), ())), preferred_element_type=F32)
        qs = (qk * (rf * (LOG2E * chans ** (-0.5)))).astype(BF16)
        qq[f] = qs
        qb[f] = jnp.sum(qs.astype(F32) * mf, axis=1, keepdims=True)

    def attend(blocks, first=False):
        for f in range(2):
            keys = [whole(zb, f) for zb in blocks]
            keys = keys[0] if len(keys) == 1 else jnp.concatenate(keys, axis=0)
            s = lax.dot_general(qq[f], keys, (((1,), (1,)), ((), ())), preferred_element_type=F32)
            s = s - qb[f]
            top = jnp.max(s, axis=1, keepdims=True)
            if not first:
                top = jnp.maximum(top, mx[f])
            p = jnp.exp2(s - top).astype(BF16)
            total = jnp.sum(p.astype(F32), axis=1, keepdims=True)
            part = jnp.dot(p, keys, preferred_element_type=F32)
            if not first:
                scale = jnp.exp2(mx[f] - top)
                total = total + den[f] * scale
                part = part + num[f] * scale
            mx[f] = top
            den[f] = total
            num[f] = part

    attend([z], True)
    z_step(last, 2)
    attend([zs(-1), zs(1)])
    z_step(last, 3)
    attend([zs(-2), zs(2)])
    z_step(last, 4)
    attend([zs(-3), zs(3)])
    attend([zs(4)])

    for f in range(2):
        mf, rf = mean[f : f + 1], rstd[f : f + 1]
        u = ((num[f] / den[f] - mf) * rf).astype(BF16)
        v = jnp.dot(u, wts[2], preferred_element_type=F32).astype(BF16)
        o = whole(z, f).astype(F32) + jnp.dot(v, wts[3], preferred_element_type=F32)
        out[f] = o.astype(BF16).reshape(out.shape[1:])

    for src, ss in sent:
        copy(src, src, ss, ss, mate, z).wait_send()


def body(latents, conv_weight, query_weight, key_weight, value_weight, out_weight):
    frames, rows_here, columns, chans = latents.shape
    taps, depth, _ = conv_weight.shape
    tokens = frames * rows_here * columns
    cols = chans // CHUNKS
    dma = pltpu.SemaphoreType.DMA
    return pl.pallas_call(
        kernel,
        out_shape=jax.ShapeDtypeStruct(latents.shape, BF16),
        in_specs=[pl.BlockSpec(memory_space=pl.ANY)] * 6,
        out_specs=pl.BlockSpec(memory_space=pltpu.VMEM),
        scratch_shapes=[
            pltpu.VMEM((4, rows_here + 2, columns, chans), BF16),
            pltpu.VMEM((3, 4, rows_here + 2, columns, chans), BF16),
            pltpu.VMEM((CHUNKS, NX, NY, NC, taps, depth, cols), BF16),
            pltpu.VMEM((CHUNKS, NZ, frames, tokens // frames, cols), BF16),
            pltpu.VMEM((tokens, cols), F32),
            pltpu.VMEM((NZ, 8, chans), F32),
            pltpu.VMEM((4, chans, chans), BF16),
            pltpu.VMEM((frames, tokens // frames, chans), BF16),
            pltpu.VMEM((frames, tokens // frames, 1), F32),
            pltpu.VMEM((frames, tokens // frames, 1), F32),
            pltpu.VMEM((frames, tokens // frames, 1), F32),
            pltpu.VMEM((frames, tokens // frames, chans), F32),
            dma((CHUNKS, 4, 4)), dma((CHUNKS, 4, 4)),
            dma((CHUNKS, 8)), dma((CHUNKS, 8)),
            dma((CHUNKS, 4, 2)), dma((CHUNKS, 4, 2)),
            dma((7,)), dma((7,)),
            dma((NZ - 1,)), dma((NZ - 1,)),
            dma((CHUNKS + 5,)),
        ],
        compiler_params=pltpu.CompilerParams(
            collective_id=0, has_side_effects=True, vmem_limit_bytes=60 * 2**20
        ),
    )(latents, conv_weight, query_weight, key_weight, value_weight, out_weight)


def solution(mesh):
    placed = (P("tm", "rows", None, None), P(None, "tm", None), P(), P(), P(), P())
    return jax.shard_map(
        body, mesh=mesh, in_specs=placed, out_specs=P("tm", "rows", None, None), check_vma=False
    )
```

time: 303 us -> 126 us (0.42)
  the two profiles are of different devices: /device:TPU:1 before, /device:TPU:32 now
where the time goes in v1:
time: 126 us; the launch traced here: 125 us
  Pallas kernels  124 us (98%)
  local copies, waits for them, and re-layouts  1.87 us (1%)
    pallas_call x1, Pallas kernels, body(): pl.pallas_call(kernel, out_shape=jax.ShapeDtypeStruct(latents.shape, BF16...  124 us

profile of v1, /device:TPU:32, one launch (start us, length us, event | category | flops | bytes accessed | tf_op | source)
XLA Modules:
  0.0 125.5 jit_solution(2986895692112694260)
XLA Ops:
  0.0 123.6 %shard_map.64 = bf16[2,4,64,512]{3,2,1,0:T(8,128)(2,1)} custom-call(bf16[2,4,64,512]{3,2,1,0:T(8,128)(2,1)} %lat.1, bf16[27,16,512]{2,1,0:T(8,128)(2,1)} %cw.1, bf16[512,512]{1,0:T(8,128)(2,1)} %wq.1, bf16[512,512]{1,0:T(8,128)(2,1)} %wk.1, bf16[512,512]{1,0:T(8,128)(2,1)} %wv.1, bf16[512,512]{1,0:T(8,128)(2,1)} %wo.1), custom_call_target="tpu_custom_call" | custom-call | tf_op jit(solution)/shard_map/pallas_call | solution.py:376
  123.6 1.9 %copy.8 = bf16[2,4,64,512]{3,2,1,0:T(8,128)(2,1)} copy(bf16[2,4,64,512]{3,2,1,0:T(8,128)(2,1)} %shard_map.64) | data formatting | bytes 1048576

commit v2 on v1

v2 whole, which is shorter than its diff:
```python
import functools

import jax
import jax.numpy as jnp
from jax import lax
from jax.experimental import pallas as pl
from jax.experimental.pallas import tpu as pltpu
from jax.sharding import PartitionSpec as P

MESH = pl.DeviceIdType.MESH
F32 = jnp.float32
BF16 = jnp.bfloat16

GROUPS = 32
EPSILON = 1e-06
LOG2E = 1.4426950408889634
NX, NY, NC, NZ = 4, 4, 2, 8
TAPS = 27
CHUNKS = 4

UNITS = (
    (0, 18, 9, 4, 2, 3),
    (0, 9, 9, 2, 1, 4),
    (0, 0, 9, 2, 1, 4),
    (1, 0, 27, 14, 5, 7),
    (2, 0, 27, 14, 5, 7),
    (3, 9, 18, 9, 4, 5),
    (3, 0, 9, 4, 2, 3),
)


def parts(u):
    _, t, m, n, up_a, up_b = UNITS[u]
    a = ((t, n), (t, up_a), (t + up_a, n - up_a))
    t, n = t + n, m - n
    return a, ((t, n), (t, up_b), (t + up_b, n - up_b))


def kernel(
    lat, cw, wq, wk, wv, wo, out,
    raw, win, w, kv, acc, st, wts, qq, qb, mx, den, num,
    w_send, w_recv, d_send, d_recv, z_send, z_recv, h_send, h_recv, s_send, s_recv, loc,
):
    tm = lax.axis_index("tm")
    z = lax.axis_index("rows")
    x, y, core = tm // (NY * NC), tm // NC % NY, tm % NC
    mate = tm + 1 - 2 * core
    ntm = NX * NY * NC

    def at(px, py):
        return (px * NY + py) * NC + core

    def xs(d):
        return (x + d + NX) % NX

    def ys(d):
        return (y + d + NY) % NY

    def zs(d):
        return (z + d + NZ) % NZ

    def copy(src, dst, ss, rs, to_tm, to_z):
        return pltpu.make_async_remote_copy(
            src_ref=src, dst_ref=dst, send_sem=ss, recv_sem=rs,
            device_id={"tm": to_tm, "rows": to_z}, device_id_type=MESH,
        )

    sent = []

    def send(src, dst, ss, rs, to_tm, to_z):
        c = copy(src, dst, ss, rs, to_tm, to_z)
        c.start()
        sent.append((src, ss))

    def arrived(ref, rs):
        copy(ref, ref, rs, rs, mate, z).wait_recv()

    chans = lat.shape[3]
    cols = chans // CHUNKS

    locals_ = [pltpu.make_async_copy(lat, raw.at[2:4, 1:5], loc.at[CHUNKS])]
    for j in range(CHUNKS):
        locals_.append(
            pltpu.make_async_copy(cw.at[:, :, j * cols : (j + 1) * cols], w.at[j, x, y, core], loc.at[j])
        )
    for i, m in enumerate((wq, wk, wv, wo)):
        locals_.append(pltpu.make_async_copy(m, wts.at[i], loc.at[CHUNKS + 1 + i]))
    for c in locals_:
        c.start()

    barrier = pltpu.get_barrier_semaphore()
    peers = [(at(xs(1), y), z), (at(xs(-1), y), z), (at(x, ys(1)), z), (at(x, ys(-1)), z)]
    peers += [(mate, z), ((tm + 1) % ntm, z), ((tm + ntm - 1) % ntm, z)]
    peers += [(tm, zs(d)) for d in range(1, NZ)]
    for ptm, pz in peers:
        pl.semaphore_signal(barrier, inc=1, device_id={"tm": ptm, "rows": pz}, device_id_type=MESH)
    pl.semaphore_wait(barrier, len(peers))

    def own(j, part):
        return cw.at[part[0] : part[0] + part[1], :, j * cols : (j + 1) * cols]

    def piece(j, px, py, part):
        return w.at[j, px, py, core, part[0] : part[0] + part[1]]

    def line_x(j, py, part):
        return w.at[j, :, py, core, part[0] : part[0] + part[1]]

    def line_y(j, px, part):
        return w.at[j, px, :, core, part[0] : part[0] + part[1]]

    def sems(u, r):
        return [(w_send.at[u, r, i], w_recv.at[u, r, i]) for i in range(4)]

    def start_1a(u):
        j = UNITS[u][0]
        (a, _, _), (b, _, _) = parts(u)
        s = sems(u, 0)
        send(own(j, a), piece(j, x, y, a), *s[0], at(xs(1), y), z)
        send(own(j, b), piece(j, x, y, b), *s[2], at(x, ys(1)), z)
        send(own(j, a), piece(j, x, y, a), *s[1], at(xs(-1), y), z)
        send(own(j, b), piece(j, x, y, b), *s[3], at(x, ys(-1)), z)

    def start_1b(u):
        j = UNITS[u][0]
        (a, a1, a2), (b, b1, b2) = parts(u)
        r = w_recv
        s = sems(u, 1)
        arrived(piece(j, xs(-1), y, a), r.at[u, 0, 0])
        src = piece(j, xs(-1), y, a1)
        send(src, src, *s[0], at(xs(1), y), z)
        arrived(piece(j, x, ys(-1), b), r.at[u, 0, 2])
        src = piece(j, x, ys(-1), b1)
        send(src, src, *s[2], at(x, ys(1)), z)
        arrived(piece(j, xs(1), y, a), r.at[u, 0, 1])
        src = piece(j, xs(1), y, a2)
        send(src, src, *s[1], at(xs(-1), y), z)
        arrived(piece(j, x, ys(1), b), r.at[u, 0, 3])
        src = piece(j, x, ys(1), b2)
        send(src, src, *s[3], at(x, ys(-1)), z)

    def to_mate(u, i, ref):
        send(ref, ref, d_send.at[u, i], d_recv.at[u, i], mate, z)

    def start_2a(u):
        j = UNITS[u][0]
        (a, a1, a2), (b, b1, b2) = parts(u)
        r = w_recv
        arrived(piece(j, xs(2), y, a1), r.at[u, 1, 0])
        arrived(piece(j, xs(2), y, a2), r.at[u, 1, 1])
        arrived(piece(j, x, ys(2), b1), r.at[u, 1, 2])
        arrived(piece(j, x, ys(2), b2), r.at[u, 1, 3])
        if u == 0 or UNITS[u - 1][0] != j:
            locals_[1 + j].wait()
        for half in range(2):
            s = sems(u, 2 + half)
            up_a, down_a = ((a1, a2), (a2, a1))[half]
            up_b, down_b = ((b1, b2), (b2, b1))[half]
            src = line_y(j, x, up_b)
            send(src, src, *s[2], at(xs(1), y), z)
            src = line_y(j, x, down_b)
            send(src, src, *s[3], at(xs(-1), y), z)
            src = line_x(j, y, up_a)
            send(src, src, *s[0], at(x, ys(1)), z)
            src = line_x(j, y, down_a)
            send(src, src, *s[1], at(x, ys(-1)), z)
        to_mate(u, 0, line_x(j, y, a))
        to_mate(u, 1, line_y(j, x, b))

    def start_2b(u):
        j = UNITS[u][0]
        (a, a1, a2), (b, b1, b2) = parts(u)
        r = w_recv
        s = sems(u, 4)
        src = line_y(j, xs(-1), b1)
        arrived(src, r.at[u, 2, 2])
        send(src, src, *s[2], at(xs(1), y), z)
        src = line_y(j, xs(1), b2)
        arrived(src, r.at[u, 2, 3])
        send(src, src, *s[3], at(xs(-1), y), z)
        src = line_x(j, ys(-1), a1)
        arrived(src, r.at[u, 2, 0])
        send(src, src, *s[0], at(x, ys(1)), z)
        src = line_x(j, ys(1), a2)
        arrived(src, r.at[u, 2, 1])
        send(src, src, *s[1], at(x, ys(-1)), z)

    def near_lines(u):
        j = UNITS[u][0]
        (a, a1, a2), (b, b1, b2) = parts(u)
        r = w_recv
        arrived(line_x(j, ys(-1), a2), r.at[u, 3, 0])
        to_mate(u, 2, line_x(j, ys(-1), a))
        arrived(line_x(j, ys(1), a1), r.at[u, 3, 1])
        to_mate(u, 3, line_x(j, ys(1), a))
        arrived(line_y(j, xs(-1), b2), r.at[u, 3, 2])
        to_mate(u, 4, line_y(j, xs(-1), b))
        arrived(line_y(j, xs(1), b1), r.at[u, 3, 3])
        to_mate(u, 5, line_y(j, xs(1), b))

    def finish_gather(u):
        j = UNITS[u][0]
        (a, a1, a2), (b, b1, b2) = parts(u)
        r = w_recv
        arrived(line_x(j, ys(2), a1), r.at[u, 4, 0])
        arrived(line_x(j, ys(2), a2), r.at[u, 4, 1])
        to_mate(u, 6, line_x(j, ys(2), a))
        arrived(line_y(j, xs(2), b1), r.at[u, 4, 2])
        arrived(line_y(j, xs(2), b2), r.at[u, 4, 3])
        to_mate(u, 7, line_y(j, xs(2), b))
        other = 1 - core
        for i, (d, along_x) in enumerate(
            ((0, True), (0, False), (-1, True), (1, True), (-1, False), (1, False), (2, True), (2, False))
        ):
            if along_x:
                ref = w.at[j, :, ys(d), other, a[0] : a[0] + a[1]]
            else:
                ref = w.at[j, xs(d), :, other, b[0] : b[0] + b[1]]
            arrived(ref, d_recv.at[u, i])

    def z_step(j, r, frames=(0, 1)):
        for f in frames:
            if r == 0:
                low = high = kv.at[j, z, f]
            elif r < 4:
                low, high = kv.at[j, zs(-r), f], kv.at[j, zs(r), f]
                arrived(low, z_recv.at[j, r - 1, 0, f])
                arrived(high, z_recv.at[j, r - 1, 1, f])
            else:
                arrived(kv.at[j, zs(4), f], z_recv.at[j, 3, f, f])
            if r < 3 or (r == 3 and f == 0):
                send(low, low, z_send.at[j, r, 0, f], z_recv.at[j, r, 0, f], tm, zs(1))
            if r < 3 or (r == 3 and f == 1):
                send(high, high, z_send.at[j, r, 1, f], z_recv.at[j, r, 1, f], tm, zs(-1))

    nxt = (tm + 1) % ntm
    start_1a(0)
    send(lat.at[:, 0], raw.at[0:2, 1], h_send.at[0], h_recv.at[0], nxt, z)
    send(lat.at[:, 3], raw.at[0:2, 4], h_send.at[1], h_recv.at[1], nxt, z)
    send(lat.at[:, 0], raw.at[2:4, 5], h_send.at[3], h_recv.at[3], tm, zs(-1))
    send(lat.at[:, 3], raw.at[2:4, 0], h_send.at[4], h_recv.at[4], tm, zs(1))
    start_1a(1)
    acc[...] = jnp.zeros_like(acc)

    col = lax.broadcasted_iota(jnp.int32, (lat.shape[2], chans), 0)

    def shift(i, carry):
        f, r = i // 6, i % 6
        outside = ((r == 0) & (z == 0)) | ((r == 5) & (z == NZ - 1)) | ((f < 2) & (tm == 0))
        keep = jnp.where(outside, 0.0, 1.0).astype(F32)
        v = raw[f, r].astype(F32) * keep
        win[1, f, r] = v.astype(BF16)
        last = lat.shape[2] - 1
        win[0, f, r] = jnp.where(col == 0, 0.0, pltpu.roll(v, 1, 0)).astype(BF16)
        win[2, f, r] = jnp.where(col == last, 0.0, pltpu.roll(v, last, 0)).astype(BF16)
        return carry

    tokens = 2 * 4 * lat.shape[2]
    per_frame = tokens // 2

    def conv(u, lo, hi):
        j, first, count_, *_ = UNITS[u]
        lags = range(first // 9, (first + count_) // 9)

        def step(i, carry):
            dr, dc = i // 3, i % 3
            sums = [None, None]
            for f in range(4):
                pairs = [(g, f - g) for g in range(2) if f - g in lags]
                if not pairs:
                    continue
                patch = win[dc, f, pl.ds(dr, 4)].reshape(per_frame, chans)
                taps = [w[j, :, :, :, 9 * lag + i].reshape(chans, cols) for _, lag in pairs]
                tap = taps[0] if len(taps) == 1 else jnp.concatenate(taps, axis=1)
                term = jnp.dot(patch, tap, preferred_element_type=F32)
                for k, (g, _) in enumerate(pairs):
                    t = term[:, k * cols : (k + 1) * cols]
                    sums[g] = t if sums[g] is None else sums[g] + t
            for g in range(2):
                acc[g] += sums[g]
            return carry

        lax.fori_loop(lo, hi, step, 0)

    lane = lax.broadcasted_iota(jnp.int32, (cols, cols), 0)
    lane2 = lax.broadcasted_iota(jnp.int32, (cols, cols), 1)
    width = chans // GROUPS
    same = (lane // width == lane2 // width).astype(F32)
    count = per_frame * width

    def group_sum(v):
        return jnp.dot(v, same, preferred_element_type=F32, precision=lax.Precision.HIGHEST)

    def finish_chunk(j):
        c = acc[...].astype(BF16)
        acc[...] = jnp.zeros_like(acc)
        kv[j, z] = c
        cf = c.astype(F32)
        mean = group_sum(jnp.sum(cf, axis=1)) * (1.0 / count)
        dev = cf - mean[:, None, :]
        st[z, 0:2, j * cols : (j + 1) * cols] = mean
        st[z, 2:4, j * cols : (j + 1) * cols] = group_sum(jnp.sum(dev * dev, axis=1))
        z_step(j, 0)

    last = CHUNKS - 1
    start_1b(0)
    start_2a(0)
    send(lat.at[:, 1:3], raw.at[0:2, 2:4], h_send.at[2], h_recv.at[2], nxt, z)
    start_1a(2)
    arrived(raw.at[2:4, 5], h_recv.at[3])
    arrived(raw.at[2:4, 0], h_recv.at[4])
    locals_[0].wait()
    arrived(raw.at[0:2, 1], h_recv.at[0])
    send(raw.at[0:2, 1], raw.at[0:2, 5], h_send.at[5], h_recv.at[5], tm, zs(-1))
    arrived(raw.at[0:2, 4], h_recv.at[1])
    send(raw.at[0:2, 4], raw.at[0:2, 0], h_send.at[6], h_recv.at[6], tm, zs(1))
    start_1b(1)
    start_2b(0)
    start_2a(1)
    near_lines(0)
    lax.fori_loop(12, 24, shift, 0)
    start_1b(2)
    start_1a(3)
    finish_gather(0)
    start_2b(1)
    start_2a(2)
    conv(0, 0, 9)
    near_lines(1)
    arrived(raw.at[0:2, 2:4], h_recv.at[2])
    arrived(raw.at[0:2, 5], h_recv.at[5])
    arrived(raw.at[0:2, 0], h_recv.at[6])
    lax.fori_loop(0, 12, shift, 0)
    start_2b(2)
    finish_gather(1)
    start_1b(3)
    conv(1, 0, 9)
    near_lines(2)
    start_2a(3)
    start_1a(4)
    finish_gather(2)
    conv(2, 0, 9)
    finish_chunk(0)
    start_2b(3)
    start_1b(4)
    start_1a(5)
    near_lines(3)
    start_2a(4)
    z_step(0, 1)
    finish_gather(3)
    conv(3, 0, 4)
    start_2b(4)
    start_1b(5)
    start_1a(6)
    z_step(0, 2)
    conv(3, 4, 6)
    near_lines(4)
    start_2a(5)
    conv(3, 6, 9)
    finish_chunk(1)
    z_step(0, 3)
    start_1b(6)
    finish_gather(4)
    conv(4, 0, 2)
    z_step(1, 1)
    start_2b(5)
    conv(4, 2, 6)
    near_lines(5)
    start_2a(6)
    z_step(0, 4)
    conv(4, 6, 9)
    z_step(1, 2)
    finish_chunk(2)
    finish_gather(5)
    start_2b(6)
    conv(5, 0, 9)
    near_lines(6)
    z_step(1, 3)
    z_step(2, 1)
    finish_gather(6)
    conv(6, 0, 9)
    finish_chunk(3)

    for d in range(1, NZ):
        send(st.at[z], st.at[z], s_send.at[d - 1], s_recv.at[d - 1], tm, zs(d))
    z_step(2, 2)
    z_step(last, 1)
    z_step(2, 3)
    z_step(1, 4)
    z_step(2, 4)
    for d in range(1, NZ):
        arrived(st.at[zs(-d)], s_recv.at[d - 1])
    for c in locals_[1 + CHUNKS :]:
        c.wait()

    means = st[:, 0:2, :]
    mean = jnp.sum(means, axis=0) * (1.0 / NZ)
    apart = means - mean[None]
    spread = jnp.sum(st[:, 2:4, :], axis=0) + count * jnp.sum(apart * apart, axis=0)
    rstd = lax.rsqrt(spread * (1.0 / (count * NZ)) + EPSILON)

    def whole(zb, f):
        return jnp.concatenate([kv[j, zb, f] for j in range(CHUNKS)], axis=1)

    for f in range(2):
        mf, rf = mean[f : f + 1], rstd[f : f + 1]
        n = ((whole(z, f).astype(F32) - mf) * rf).astype(BF16)
        q = jnp.dot(n, wts[0], preferred_element_type=F32).astype(BF16)
        qk = lax.dot_general(q, wts[1], (((1,), (1,)), ((), ())), preferred_element_type=F32)
        qs = (qk * (rf * (LOG2E * chans ** (-0.5)))).astype(BF16)
        qq[f] = qs
        qb[f] = jnp.sum(qs.astype(F32) * mf, axis=1, keepdims=True)

    def attend(blocks, first=False):
        for f in range(2):
            keys = [whole(zb, f) for zb in blocks]
            keys = keys[0] if len(keys) == 1 else jnp.concatenate(keys, axis=0)
            s = lax.dot_general(qq[f], keys, (((1,), (1,)), ((), ())), preferred_element_type=F32)
            s = s - qb[f]
            top = jnp.max(s, axis=1, keepdims=True)
            if not first:
                top = jnp.maximum(top, mx[f])
            p = jnp.exp2(s - top).astype(BF16)
            total = jnp.sum(p.astype(F32), axis=1, keepdims=True)
            part = jnp.dot(p, keys, preferred_element_type=F32)
            if not first:
                scale = jnp.exp2(mx[f] - top)
                total = total + den[f] * scale
                part = part + num[f] * scale
            mx[f] = top
            den[f] = total
            num[f] = part

    attend([z], True)
    z_step(last, 2)
    attend([zs(-1), zs(1)])
    z_step(last, 3)
    attend([zs(-2), zs(2)])
    z_step(last, 4)
    attend([zs(-3), zs(3)])
    attend([zs(4)])

    for f in range(2):
        mf, rf = mean[f : f + 1], rstd[f : f + 1]
        u = ((num[f] / den[f] - mf) * rf).astype(BF16)
        v = jnp.dot(u, wts[2], preferred_element_type=F32).astype(BF16)
        o = whole(z, f).astype(F32) + jnp.dot(v, wts[3], preferred_element_type=F32)
        out[f] = o.astype(BF16).reshape(out.shape[1:])

    for src, ss in sent:
        copy(src, src, ss, ss, mate, z).wait_send()


def body(latents, conv_weight, query_weight, key_weight, value_weight, out_weight):
    frames, rows_here, columns, chans = latents.shape
    taps, depth, _ = conv_weight.shape
    tokens = frames * rows_here * columns
    cols = chans // CHUNKS
    dma = pltpu.SemaphoreType.DMA
    return pl.pallas_call(
        kernel,
        out_shape=jax.ShapeDtypeStruct(latents.shape, BF16),
        in_specs=[pl.BlockSpec(memory_space=pl.ANY)] * 6,
        out_specs=pl.BlockSpec(memory_space=pltpu.VMEM),
        scratch_shapes=[
            pltpu.VMEM((4, rows_here + 2, columns, chans), BF16),
            pltpu.VMEM((3, 4, rows_here + 2, columns, chans), BF16),
            pltpu.VMEM((CHUNKS, NX, NY, NC, taps, depth, cols), BF16),
            pltpu.VMEM((CHUNKS, NZ, frames, tokens // frames, cols), BF16),
            pltpu.VMEM((frames, tokens // frames, cols), F32),
            pltpu.VMEM((NZ, 8, chans), F32),
            pltpu.VMEM((4, chans, chans), BF16),
            pltpu.VMEM((frames, tokens // frames, chans), BF16),
            pltpu.VMEM((frames, tokens // frames, 1), F32),
            pltpu.VMEM((frames, tokens // frames, 1), F32),
            pltpu.VMEM((frames, tokens // frames, 1), F32),
            pltpu.VMEM((frames, tokens // frames, chans), F32),
            dma((len(UNITS), 5, 4)), dma((len(UNITS), 5, 4)),
            dma((len(UNITS), 8)), dma((len(UNITS), 8)),
            dma((CHUNKS, 4, 2, 2)), dma((CHUNKS, 4, 2, 2)),
            dma((7,)), dma((7,)),
            dma((NZ - 1,)), dma((NZ - 1,)),
            dma((CHUNKS + 5,)),
        ],
        compiler_params=pltpu.CompilerParams(
            collective_id=0, has_side_effects=True, vmem_limit_bytes=60 * 2**20
        ),
    )(latents, conv_weight, query_weight, key_weight, value_weight, out_weight)


def solution(mesh):
    placed = (P("tm", "rows", None, None), P(None, "tm", None), P(), P(), P(), P())
    return jax.shard_map(
        body, mesh=mesh, in_specs=placed, out_specs=P("tm", "rows", None, None), check_vma=False
    )
```

time: 126 us -> 117 us (0.929)
  the two profiles are of different devices: /device:TPU:32 before, /device:TPU:1 now
where the time goes in v2:
time: 117 us; the launch traced here: 116 us
  Pallas kernels  114 us (97%)
  local copies, waits for them, and re-layouts  1.87 us (2%)
    pallas_call x1, Pallas kernels, body(): pl.pallas_call(kernel, out_shape=jax.ShapeDtypeStruct(latents.shape, BF16...  114 us

profile of v2, /device:TPU:1, one launch (start us, length us, event | category | flops | bytes accessed | tf_op | source)
XLA Modules:
  0.0 116.1 jit_solution(13008151950407175374)
XLA Ops:
  0.0 114.2 %shard_map.64 = bf16[2,4,64,512]{3,2,1,0:T(8,128)(2,1)} custom-call(bf16[2,4,64,512]{3,2,1,0:T(8,128)(2,1)} %lat.1, bf16[27,16,512]{2,1,0:T(8,128)(2,1)} %cw.1, bf16[512,512]{1,0:T(8,128)(2,1)} %wq.1, bf16[512,512]{1,0:T(8,128)(2,1)} %wk.1, bf16[512,512]{1,0:T(8,128)(2,1)} %wv.1, bf16[512,512]{1,0:T(8,128)(2,1)} %wo.1), custom_call_target="tpu_custom_call" | custom-call | tf_op jit(solution)/shard_map/pallas_call | solution.py:458
  114.2 1.9 %copy.8 = bf16[2,4,64,512]{3,2,1,0:T(8,128)(2,1)} copy(bf16[2,4,64,512]{3,2,1,0:T(8,128)(2,1)} %shard_map.64) | data formatting | bytes 1048576

commit v3 on v2

--- a/solution.py
+++ b/solution.py
@@ -20,8 +20,7 @@
 
 UNITS = (
     (0, 18, 9, 4, 2, 3),
-    (0, 9, 9, 2, 1, 4),
-    (0, 0, 9, 2, 1, 4),
+    (0, 0, 18, 4, 1, 7),
     (1, 0, 27, 14, 5, 7),
     (2, 0, 27, 14, 5, 7),
     (3, 9, 18, 9, 4, 5),
@@ -72,6 +71,11 @@
         c.start()
         sent.append((src, ss))
 
+    def flush():
+        for src, ss in sent:
+            copy(src, src, ss, ss, mate, z).wait_send()
+        sent.clear()
+
     def arrived(ref, rs):
         copy(ref, ref, rs, rs, mate, z).wait_recv()
 
@@ -85,8 +89,8 @@
         )
     for i, m in enumerate((wq, wk, wv, wo)):
         locals_.append(pltpu.make_async_copy(m, wts.at[i], loc.at[CHUNKS + 1 + i]))
-    for c in locals_:
-        c.start()
+    for i in (1, 0, *range(2, len(locals_))):
+        locals_[i].start()
 
     barrier = pltpu.get_barrier_semaphore()
     peers = [(at(xs(1), y), z), (at(xs(-1), y), z), (at(x, ys(1)), z), (at(x, ys(-1)), z)]
@@ -96,9 +100,6 @@
         pl.semaphore_signal(barrier, inc=1, device_id={"tm": ptm, "rows": pz}, device_id_type=MESH)
     pl.semaphore_wait(barrier, len(peers))
 
-    def own(j, part):
-        return cw.at[part[0] : part[0] + part[1], :, j * cols : (j + 1) * cols]
-
     def piece(j, px, py, part):
         return w.at[j, px, py, core, part[0] : part[0] + part[1]]
 
@@ -115,10 +116,14 @@
         j = UNITS[u][0]
         (a, _, _), (b, _, _) = parts(u)
         s = sems(u, 0)
-        send(own(j, a), piece(j, x, y, a), *s[0], at(xs(1), y), z)
-        send(own(j, b), piece(j, x, y, b), *s[2], at(x, ys(1)), z)
-        send(own(j, a), piece(j, x, y, a), *s[1], at(xs(-1), y), z)
-        send(own(j, b), piece(j, x, y, b), *s[3], at(x, ys(-1)), z)
+        if u == 0 or UNITS[u - 1][0] != j:
+            locals_[1 + j].wait()
+        src = piece(j, x, y, a)
+        send(src, src, *s[0], at(xs(1), y), z)
+        send(src, src, *s[1], at(xs(-1), y), z)
+        src = piece(j, x, y, b)
+        send(src, src, *s[2], at(x, ys(1)), z)
+        send(src, src, *s[3], at(x, ys(-1)), z)
 
     def start_1b(u):
         j = UNITS[u][0]
@@ -149,8 +154,6 @@
         arrived(piece(j, xs(2), y, a2), r.at[u, 1, 1])
         arrived(piece(j, x, ys(2), b1), r.at[u, 1, 2])
         arrived(piece(j, x, ys(2), b2), r.at[u, 1, 3])
-        if u == 0 or UNITS[u - 1][0] != j:
-            locals_[1 + j].wait()
         for half in range(2):
             s = sems(u, 2 + half)
             up_a, down_a = ((a1, a2), (a2, a1))[half]
@@ -234,11 +237,9 @@
 
     nxt = (tm + 1) % ntm
     start_1a(0)
-    send(lat.at[:, 0], raw.at[0:2, 1], h_send.at[0], h_recv.at[0], nxt, z)
-    send(lat.at[:, 3], raw.at[0:2, 4], h_send.at[1], h_recv.at[1], nxt, z)
+    start_1a(1)
     send(lat.at[:, 0], raw.at[2:4, 5], h_send.at[3], h_recv.at[3], tm, zs(-1))
     send(lat.at[:, 3], raw.at[2:4, 0], h_send.at[4], h_recv.at[4], tm, zs(1))
-    start_1a(1)
     acc[...] = jnp.zeros_like(acc)
 
     col = lax.broadcasted_iota(jnp.int32, (lat.shape[2], chans), 0)
@@ -302,90 +303,79 @@
         z_step(j, 0)
 
     last = CHUNKS - 1
+
+    def start_group(u):
+        if u + 2 < len(UNITS):
+            start_1a(u + 2)
+        if u + 1 < len(UNITS):
+            start_1b(u + 1)
+        start_2a(u)
+
     start_1b(0)
-    start_2a(0)
-    send(lat.at[:, 1:3], raw.at[0:2, 2:4], h_send.at[2], h_recv.at[2], nxt, z)
-    start_1a(2)
+    start_group(0)
+    send(lat.at[:, 0], raw.at[0:2, 1], h_send.at[0], h_recv.at[0], nxt, z)
+    send(lat.at[:, 3], raw.at[0:2, 4], h_send.at[1], h_recv.at[1], nxt, z)
     arrived(raw.at[2:4, 5], h_recv.at[3])
     arrived(raw.at[2:4, 0], h_recv.at[4])
     locals_[0].wait()
+    lax.fori_loop(12, 24, shift, 0)
+    start_2b(0)
+    send(lat.at[:, 1:3], raw.at[0:2, 2:4], h_send.at[2], h_recv.at[2], nxt, z)
+    start_group(1)
+    near_lines(0)
     arrived(raw.at[0:2, 1], h_recv.at[0])
     send(raw.at[0:2, 1], raw.at[0:2, 5], h_send.at[5], h_recv.at[5], tm, zs(-1))
     arrived(raw.at[0:2, 4], h_recv.at[1])
     send(raw.at[0:2, 4], raw.at[0:2, 0], h_send.at[6], h_recv.at[6], tm, zs(1))
-    start_1b(1)
-    start_2b(0)
-    start_2a(1)
-    near_lines(0)
-    lax.fori_loop(12, 24, shift, 0)
-    start_1b(2)
-    start_1a(3)
     finish_gather(0)
     start_2b(1)
-    start_2a(2)
+    start_group(2)
     conv(0, 0, 9)
     near_lines(1)
     arrived(raw.at[0:2, 2:4], h_recv.at[2])
     arrived(raw.at[0:2, 5], h_recv.at[5])
     arrived(raw.at[0:2, 0], h_recv.at[6])
     lax.fori_loop(0, 12, shift, 0)
+    finish_gather(1)
+    conv(1, 0, 5)
     start_2b(2)
-    finish_gather(1)
-    start_1b(3)
-    conv(1, 0, 9)
+    start_group(3)
+    conv(1, 5, 9)
+    finish_chunk(0)
     near_lines(2)
-    start_2a(3)
-    start_1a(4)
+    z_step(0, 1)
     finish_gather(2)
-    conv(2, 0, 9)
-    finish_chunk(0)
+    conv(2, 0, 3)
     start_2b(3)
-    start_1b(4)
-    start_1a(5)
+    start_group(4)
+    conv(2, 3, 9)
+    z_step(0, 2)
+    finish_chunk(1)
     near_lines(3)
-    start_2a(4)
-    z_step(0, 1)
+    start_2b(4)
+    start_group(5)
+    z_step(0, 3)
     finish_gather(3)
-    conv(3, 0, 4)
-    start_2b(4)
-    start_1b(5)
-    start_1a(6)
-    z_step(0, 2)
-    conv(3, 4, 6)
+    z_step(1, 1)
+    conv(3, 0, 5)
     near_lines(4)
-    start_2a(5)
-    conv(3, 6, 9)
-    finish_chunk(1)
-    z_step(0, 3)
-    start_1b(6)
-    finish_gather(4)
-    conv(4, 0, 2)
-    z_step(1, 1)
     start_2b(5)
-    conv(4, 2, 6)
-    near_lines(5)
-    start_2a(6)
-    z_step(0, 4)
-    conv(4, 6, 9)
+    conv(3, 5, 9)
     z_step(1, 2)
     finish_chunk(2)
-    finish_gather(5)
-    start_2b(6)
-    conv(5, 0, 9)
-    near_lines(6)
+    near_lines(5)
+    finish_gather(4)
+    conv(4, 0, 9)
     z_step(1, 3)
     z_step(2, 1)
-    finish_gather(6)
-    conv(6, 0, 9)
+    finish_gather(5)
+    conv(5, 0, 9)
     finish_chunk(3)
 
     for d in range(1, NZ):
         send(st.at[z], st.at[z], s_send.at[d - 1], s_recv.at[d - 1], tm, zs(d))
     z_step(2, 2)
     z_step(last, 1)
-    z_step(2, 3)
-    z_step(1, 4)
-    z_step(2, 4)
     for d in range(1, NZ):
         arrived(st.at[zs(-d)], s_recv.at[d - 1])
     for c in locals_[1 + CHUNKS :]:
@@ -429,13 +419,16 @@
             den[f] = total
             num[f] = part
 
+    z_step(2, 3)
     attend([z], True)
     z_step(last, 2)
     attend([zs(-1), zs(1)])
+    flush()
     z_step(last, 3)
     attend([zs(-2), zs(2)])
-    z_step(last, 4)
     attend([zs(-3), zs(3)])
+    for j in range(CHUNKS):
+        z_step(j, 4)
     attend([zs(4)])
 
     for f in range(2):
@@ -445,8 +438,7 @@
         o = whole(z, f).astype(F32) + jnp.dot(v, wts[3], preferred_element_type=F32)
         out[f] = o.astype(BF16).reshape(out.shape[1:])
 
-    for src, ss in sent:
-        copy(src, src, ss, ss, mate, z).wait_send()
+    flush()
 
 
 def body(latents, conv_weight, query_weight, key_weight, value_weight, out_weight):

time: 117 us -> 105 us (0.90)
  Pallas kernels: 114 us -> 103 us
    pallas_call x1, Pallas kernels: 114 us -> 103 us  [body(): pl.pallas_call(kernel, out_shape=jax.ShapeDtypeStruct(latents.shape, BF16...]
where the time goes in v3:
time: 105 us
  Pallas kernels  103 us (98%)
  local copies, waits for them, and re-layouts  1.87 us (2%)
    pallas_call x1, Pallas kernels, body(): pl.pallas_call(kernel, out_shape=jax.ShapeDtypeStruct(latents.shape, BF16...  103 us

profile of v3, /device:TPU:1, one launch (start us, length us, event | category | flops | bytes accessed | tf_op | source)
XLA Modules:
  0.0 104.7 jit_solution(7289119547292855233)
XLA Ops:
  0.0 102.8 %shard_map.64 = bf16[2,4,64,512]{3,2,1,0:T(8,128)(2,1)} custom-call(bf16[2,4,64,512]{3,2,1,0:T(8,128)(2,1)} %lat.1, bf16[27,16,512]{2,1,0:T(8,128)(2,1)} %cw.1, bf16[512,512]{1,0:T(8,128)(2,1)} %wq.1, bf16[512,512]{1,0:T(8,128)(2,1)} %wk.1, bf16[512,512]{1,0:T(8,128)(2,1)} %wv.1, bf16[512,512]{1,0:T(8,128)(2,1)} %wo.1), custom_call_target="tpu_custom_call" | custom-call | tf_op jit(solution)/shard_map/pallas_call | solution.py:450
  102.8 1.9 %copy.8 = bf16[2,4,64,512]{3,2,1,0:T(8,128)(2,1)} copy(bf16[2,4,64,512]{3,2,1,0:T(8,128)(2,1)} %shard_map.64) | data formatting | bytes 1048576

commit v4 on v3

--- a/solution.py
+++ b/solution.py
@@ -19,8 +19,7 @@
 CHUNKS = 4
 
 UNITS = (
-    (0, 18, 9, 4, 2, 3),
-    (0, 0, 18, 4, 1, 7),
+    (0, 0, 27, 14, 4, 4),
     (1, 0, 27, 14, 5, 7),
     (2, 0, 27, 14, 5, 7),
     (3, 9, 18, 9, 4, 5),
@@ -38,7 +37,7 @@
 def kernel(
     lat, cw, wq, wk, wv, wo, out,
     raw, win, w, kv, acc, st, wts, qq, qb, mx, den, num,
-    w_send, w_recv, d_send, d_recv, z_send, z_recv, h_send, h_recv, s_send, s_recv, loc,
+    w_send, w_recv, z_send, z_recv, h_send, h_recv, s_send, s_recv, loc,
 ):
     tm = lax.axis_index("tm")
     z = lax.axis_index("rows")
@@ -64,17 +63,15 @@
             device_id={"tm": to_tm, "rows": to_z}, device_id_type=MESH,
         )
 
-    sent = []
+    pending = []
 
     def send(src, dst, ss, rs, to_tm, to_z):
-        c = copy(src, dst, ss, rs, to_tm, to_z)
-        c.start()
-        sent.append((src, ss))
+        copy(src, dst, ss, rs, to_tm, to_z).start()
 
     def flush():
-        for src, ss in sent:
-            copy(src, src, ss, ss, mate, z).wait_send()
-        sent.clear()
+        for ref, ss in pending:
+            copy(ref, ref, ss, ss, mate, z).wait_send()
+        pending.clear()
 
     def arrived(ref, rs):
         copy(ref, ref, rs, rs, mate, z).wait_recv()
@@ -93,7 +90,7 @@
         locals_[i].start()
 
     barrier = pltpu.get_barrier_semaphore()
-    peers = [(at(xs(1), y), z), (at(xs(-1), y), z), (at(x, ys(1)), z), (at(x, ys(-1)), z)]
+    peers = [(at(xs(d), y), z) for d in range(1, NX)] + [(at(x, ys(d)), z) for d in range(1, NY)]
     peers += [(mate, z), ((tm + 1) % ntm, z), ((tm + ntm - 1) % ntm, z)]
     peers += [(tm, zs(d)) for d in range(1, NZ)]
     for ptm, pz in peers:
@@ -109,14 +106,22 @@
     def line_y(j, px, part):
         return w.at[j, px, :, core, part[0] : part[0] + part[1]]
 
-    def sems(u, r):
-        return [(w_send.at[u, r, i], w_recv.at[u, r, i]) for i in range(4)]
+    def block(u, *lead):
+        j, t, m, *_ = UNITS[u]
+        return w.at[(j, *lead, core, slice(t, t + m))]
+
+    everything = slice(None)
+    sizes = (0, slice(0, 2)), (0, 0), (slice(0, 2), everything), (0, everything), (everything, everything)
+
+    def sems(u, r, base):
+        pending.append((block(u, *sizes[r]), w_send.at[u, r]))
+        return [(w_send.at[u, r], w_recv.at[u, base + i]) for i in range(4)]
 
     def start_1a(u):
         j = UNITS[u][0]
         (a, _, _), (b, _, _) = parts(u)
-        s = sems(u, 0)
-        if u == 0 or UNITS[u - 1][0] != j:
+        s = sems(u, 0, 0)
+        if UNITS[u - 1][0] != j:
             locals_[1 + j].wait()
         src = piece(j, x, y, a)
         send(src, src, *s[0], at(xs(1), y), z)
@@ -124,38 +129,49 @@
         src = piece(j, x, y, b)
         send(src, src, *s[2], at(x, ys(1)), z)
         send(src, src, *s[3], at(x, ys(-1)), z)
+        if u == 0:
+            s = sems(u, 1, 4)
+            send(src, src, *s[1], at(x, ys(2)), z)
+            src = piece(j, x, y, a)
+            send(src, src, *s[0], at(xs(2), y), z)
+
+    def from_mate(u):
+        j, t, m, *_ = UNITS[u]
+        arrived(w.at[j, :, :, 1 - core, t : t + m], w_recv.at[u, 16])
+
+    def to_mate(u, ref):
+        send(ref, ref, w_send.at[u, 4], w_recv.at[u, 16], mate, z)
 
     def start_1b(u):
         j = UNITS[u][0]
         (a, a1, a2), (b, b1, b2) = parts(u)
         r = w_recv
-        s = sems(u, 1)
-        arrived(piece(j, xs(-1), y, a), r.at[u, 0, 0])
+        s = sems(u, 1, 4)
+        arrived(piece(j, xs(-1), y, a), r.at[u, 0])
         src = piece(j, xs(-1), y, a1)
         send(src, src, *s[0], at(xs(1), y), z)
-        arrived(piece(j, x, ys(-1), b), r.at[u, 0, 2])
+        arrived(piece(j, x, ys(-1), b), r.at[u, 2])
         src = piece(j, x, ys(-1), b1)
-        send(src, src, *s[2], at(x, ys(1)), z)
-        arrived(piece(j, xs(1), y, a), r.at[u, 0, 1])
+        send(src, src, *s[1], at(x, ys(1)), z)
+        arrived(piece(j, xs(1), y, a), r.at[u, 1])
         src = piece(j, xs(1), y, a2)
-        send(src, src, *s[1], at(xs(-1), y), z)
-        arrived(piece(j, x, ys(1), b), r.at[u, 0, 3])
+        send(src, src, *s[0], at(xs(-1), y), z)
+        arrived(piece(j, x, ys(1), b), r.at[u, 3])
         src = piece(j, x, ys(1), b2)
-        send(src, src, *s[3], at(x, ys(-1)), z)
-
-    def to_mate(u, i, ref):
-        send(ref, ref, d_send.at[u, i], d_recv.at[u, i], mate, z)
+        send(src, src, *s[1], at(x, ys(-1)), z)
 
     def start_2a(u):
         j = UNITS[u][0]
         (a, a1, a2), (b, b1, b2) = parts(u)
         r = w_recv
-        arrived(piece(j, xs(2), y, a1), r.at[u, 1, 0])
-        arrived(piece(j, xs(2), y, a2), r.at[u, 1, 1])
-        arrived(piece(j, x, ys(2), b1), r.at[u, 1, 2])
-        arrived(piece(j, x, ys(2), b2), r.at[u, 1, 3])
+        if u == 0:
+            for i, d in enumerate((-1, 1)):
+                arrived(piece(j, xs(d), y, a), r.at[u, i])
+                arrived(piece(j, x, ys(d), b), r.at[u, 2 + i])
+        arrived(piece(j, xs(2), y, a), r.at[u, 4])
+        arrived(piece(j, x, ys(2), b), r.at[u, 5])
         for half in range(2):
-            s = sems(u, 2 + half)
+            s = [(w_send.at[u, 2], w_recv.at[u, 6 + 4 * half + i]) for i in range(4)]
             up_a, down_a = ((a1, a2), (a2, a1))[half]
             up_b, down_b = ((b1, b2), (b2, b1))[half]
             src = line_y(j, x, up_b)
@@ -166,61 +182,54 @@
             send(src, src, *s[0], at(x, ys(1)), z)
             src = line_x(j, y, down_a)
             send(src, src, *s[1], at(x, ys(-1)), z)
-        to_mate(u, 0, line_x(j, y, a))
-        to_mate(u, 1, line_y(j, x, b))
+        pending.append((block(u, *sizes[2]), w_send.at[u, 2]))
+        pending.append((block(u, *sizes[4]), w_send.at[u, 4]))
+        to_mate(u, line_x(j, y, a))
+        to_mate(u, line_y(j, x, b))
 
     def start_2b(u):
         j = UNITS[u][0]
         (a, a1, a2), (b, b1, b2) = parts(u)
         r = w_recv
-        s = sems(u, 4)
+        s = sems(u, 3, 14)
         src = line_y(j, xs(-1), b1)
-        arrived(src, r.at[u, 2, 2])
-        send(src, src, *s[2], at(xs(1), y), z)
+        arrived(src, r.at[u, 8])
+        send(src, src, *s[1], at(xs(1), y), z)
         src = line_y(j, xs(1), b2)
-        arrived(src, r.at[u, 2, 3])
-        send(src, src, *s[3], at(xs(-1), y), z)
+        arrived(src, r.at[u, 9])
+        send(src, src, *s[1], at(xs(-1), y), z)
         src = line_x(j, ys(-1), a1)
-        arrived(src, r.at[u, 2, 0])
+        arrived(src, r.at[u, 6])
         send(src, src, *s[0], at(x, ys(1)), z)
         src = line_x(j, ys(1), a2)
-        arrived(src, r.at[u, 2, 1])
-        send(src, src, *s[1], at(x, ys(-1)), z)
+        arrived(src, r.at[u, 7])
+        send(src, src, *s[0], at(x, ys(-1)), z)
 
     def near_lines(u):
         j = UNITS[u][0]
         (a, a1, a2), (b, b1, b2) = parts(u)
         r = w_recv
-        arrived(line_x(j, ys(-1), a2), r.at[u, 3, 0])
-        to_mate(u, 2, line_x(j, ys(-1), a))
-        arrived(line_x(j, ys(1), a1), r.at[u, 3, 1])
-        to_mate(u, 3, line_x(j, ys(1), a))
-        arrived(line_y(j, xs(-1), b2), r.at[u, 3, 2])
-        to_mate(u, 4, line_y(j, xs(-1), b))
-        arrived(line_y(j, xs(1), b1), r.at[u, 3, 3])
-        to_mate(u, 5, line_y(j, xs(1), b))
+        arrived(line_x(j, ys(-1), a2), r.at[u, 10])
+        to_mate(u, line_x(j, ys(-1), a))
+        arrived(line_x(j, ys(1), a1), r.at[u, 11])
+        to_mate(u, line_x(j, ys(1), a))
+        arrived(line_y(j, xs(-1), b2), r.at[u, 12])
+        to_mate(u, line_y(j, xs(-1), b))
+        arrived(line_y(j, xs(1), b1), r.at[u, 13])
+        to_mate(u, line_y(j, xs(1), b))
 
     def finish_gather(u):
         j = UNITS[u][0]
         (a, a1, a2), (b, b1, b2) = parts(u)
-        r = w_recv
-        arrived(line_x(j, ys(2), a1), r.at[u, 4, 0])
-        arrived(line_x(j, ys(2), a2), r.at[u, 4, 1])
-        to_mate(u, 6, line_x(j, ys(2), a))
-        arrived(line_y(j, xs(2), b1), r.at[u, 4, 2])
-        arrived(line_y(j, xs(2), b2), r.at[u, 4, 3])
-        to_mate(u, 7, line_y(j, xs(2), b))
-        other = 1 - core
-        for i, (d, along_x) in enumerate(
-            ((0, True), (0, False), (-1, True), (1, True), (-1, False), (1, False), (2, True), (2, False))
-        ):
-            if along_x:
-                ref = w.at[j, :, ys(d), other, a[0] : a[0] + a[1]]
-            else:
-                ref = w.at[j, xs(d), :, other, b[0] : b[0] + b[1]]
-            arrived(ref, d_recv.at[u, i])
+        arrived(line_x(j, ys(2), a), w_recv.at[u, 14])
+        to_mate(u, line_x(j, ys(2), a))
+        arrived(line_y(j, xs(2), b), w_recv.at[u, 15])
+        to_mate(u, line_y(j, xs(2), b))
+        from_mate(u)
 
     def z_step(j, r, frames=(0, 1)):
+        if r == 3:
+            pending.append((kv.at[j, 0 : NZ - 1], z_send.at[j]))
         for f in frames:
             if r == 0:
                 low = high = kv.at[j, z, f]
@@ -231,15 +240,18 @@
             else:
                 arrived(kv.at[j, zs(4), f], z_recv.at[j, 3, f, f])
             if r < 3 or (r == 3 and f == 0):
-                send(low, low, z_send.at[j, r, 0, f], z_recv.at[j, r, 0, f], tm, zs(1))
+                send(low, low, z_send.at[j], z_recv.at[j, r, 0, f], tm, zs(1))
             if r < 3 or (r == 3 and f == 1):
-                send(high, high, z_send.at[j, r, 1, f], z_recv.at[j, r, 1, f], tm, zs(-1))
+                send(high, high, z_send.at[j], z_recv.at[j, r, 1, f], tm, zs(-1))
 
     nxt = (tm + 1) % ntm
     start_1a(0)
-    start_1a(1)
     send(lat.at[:, 0], raw.at[2:4, 5], h_send.at[3], h_recv.at[3], tm, zs(-1))
     send(lat.at[:, 3], raw.at[2:4, 0], h_send.at[4], h_recv.at[4], tm, zs(1))
+    send(lat.at[:, 0], raw.at[0:2, 1], h_send.at[0], h_recv.at[0], nxt, z)
+    send(lat.at[:, 3], raw.at[0:2, 4], h_send.at[1], h_recv.at[1], nxt, z)
+    send(lat.at[:, 1:3], raw.at[0:2, 2:4], h_send.at[2], h_recv.at[2], nxt, z)
+    start_1a(1)
     acc[...] = jnp.zeros_like(acc)
 
     col = lax.broadcasted_iota(jnp.int32, (lat.shape[2], chans), 0)
@@ -303,81 +315,72 @@
         z_step(j, 0)
 
     last = CHUNKS - 1
-
-    def start_group(u):
-        if u + 2 < len(UNITS):
-            start_1a(u + 2)
-        if u + 1 < len(UNITS):
-            start_1b(u + 1)
-        start_2a(u)
-
-    start_1b(0)
-    start_group(0)
-    send(lat.at[:, 0], raw.at[0:2, 1], h_send.at[0], h_recv.at[0], nxt, z)
-    send(lat.at[:, 3], raw.at[0:2, 4], h_send.at[1], h_recv.at[1], nxt, z)
+    start_2a(0)
     arrived(raw.at[2:4, 5], h_recv.at[3])
     arrived(raw.at[2:4, 0], h_recv.at[4])
     locals_[0].wait()
     lax.fori_loop(12, 24, shift, 0)
-    start_2b(0)
-    send(lat.at[:, 1:3], raw.at[0:2, 2:4], h_send.at[2], h_recv.at[2], nxt, z)
-    start_group(1)
-    near_lines(0)
     arrived(raw.at[0:2, 1], h_recv.at[0])
     send(raw.at[0:2, 1], raw.at[0:2, 5], h_send.at[5], h_recv.at[5], tm, zs(-1))
     arrived(raw.at[0:2, 4], h_recv.at[1])
     send(raw.at[0:2, 4], raw.at[0:2, 0], h_send.at[6], h_recv.at[6], tm, zs(1))
+    start_1b(1)
+    start_1a(2)
+    start_2b(0)
+    start_2a(1)
+    near_lines(0)
+    start_1b(2)
+    start_1a(3)
+    arrived(raw.at[0:2, 5], h_recv.at[5])
+    arrived(raw.at[0:2, 0], h_recv.at[6])
+    arrived(raw.at[0:2, 2:4], h_recv.at[2])
+    lax.fori_loop(0, 12, shift, 0)
+    pending.extend((raw.at[0:2, 0], h_send.at[i]) for i in (0, 1, 3, 4, 5, 6))
+    pending.append((raw.at[0:2, 0:2], h_send.at[2]))
     finish_gather(0)
     start_2b(1)
-    start_group(2)
+    start_2a(2)
+    start_1b(3)
+    start_1a(4)
     conv(0, 0, 9)
+    finish_chunk(0)
     near_lines(1)
-    arrived(raw.at[0:2, 2:4], h_recv.at[2])
-    arrived(raw.at[0:2, 5], h_recv.at[5])
-    arrived(raw.at[0:2, 0], h_recv.at[6])
-    lax.fori_loop(0, 12, shift, 0)
+    start_1b(4)
     finish_gather(1)
-    conv(1, 0, 5)
     start_2b(2)
-    start_group(3)
-    conv(1, 5, 9)
-    finish_chunk(0)
+    start_2a(3)
+    z_step(0, 1)
+    conv(1, 0, 6)
     near_lines(2)
-    z_step(0, 1)
-    finish_gather(2)
-    conv(2, 0, 3)
-    start_2b(3)
-    start_group(4)
-    conv(2, 3, 9)
+    start_2a(4)
+    conv(1, 6, 9)
     z_step(0, 2)
     finish_chunk(1)
+    start_2b(3)
+    finish_gather(2)
+    z_step(0, 3)
+    z_step(1, 1)
+    conv(2, 0, 5)
     near_lines(3)
     start_2b(4)
-    start_group(5)
-    z_step(0, 3)
-    finish_gather(3)
-    z_step(1, 1)
-    conv(3, 0, 5)
-    near_lines(4)
-    start_2b(5)
-    conv(3, 5, 9)
+    conv(2, 5, 9)
     z_step(1, 2)
     finish_chunk(2)
-    near_lines(5)
+    finish_gather(3)
+    near_lines(4)
+    conv(3, 0, 9)
+    z_step(1, 3)
+    z_step(2, 1)
     finish_gather(4)
     conv(4, 0, 9)
-    z_step(1, 3)
-    z_step(2, 1)
-    finish_gather(5)
-    conv(5, 0, 9)
     finish_chunk(3)
 
     for d in range(1, NZ):
-        send(st.at[z], st.at[z], s_send.at[d - 1], s_recv.at[d - 1], tm, zs(d))
+        send(st.at[z], st.at[z], s_send.at[0], s_recv.at[0], tm, zs(d))
+    pending.append((st.at[0 : NZ - 1], s_send.at[0]))
     z_step(2, 2)
     z_step(last, 1)
-    for d in range(1, NZ):
-        arrived(st.at[zs(-d)], s_recv.at[d - 1])
+    arrived(st.at[0 : NZ - 1], s_recv.at[0])
     for c in locals_[1 + CHUNKS :]:
         c.wait()
 
@@ -465,11 +468,10 @@
             pltpu.VMEM((frames, tokens // frames, 1), F32),
             pltpu.VMEM((frames, tokens // frames, 1), F32),
             pltpu.VMEM((frames, tokens // frames, chans), F32),
-            dma((len(UNITS), 5, 4)), dma((len(UNITS), 5, 4)),
-            dma((len(UNITS), 8)), dma((len(UNITS), 8)),
-            dma((CHUNKS, 4, 2, 2)), dma((CHUNKS, 4, 2, 2)),
+            dma((len(UNITS), 5)), dma((len(UNITS), 17)),
+            dma((CHUNKS,)), dma((CHUNKS, 4, 2, 2)),
             dma((7,)), dma((7,)),
-            dma((NZ - 1,)), dma((NZ - 1,)),
+            dma((1,)), dma((1,)),
             dma((CHUNKS + 5,)),
         ],
         compiler_params=pltpu.CompilerParams(

time: 105 us -> 101 us (0.962)
  Pallas kernels: 103 us -> 98.3 us
    pallas_call x1, Pallas kernels: 103 us -> 98.3 us  [body(): pl.pallas_call(kernel, out_shape=jax.ShapeDtypeStruct(latents.shape, BF16...]
where the time goes in v4:
time: 101 us; the launch traced here: 100 us
  Pallas kernels  98.3 us (97%)
  local copies, waits for them, and re-layouts  1.87 us (2%)
    pallas_call x1, Pallas kernels, body(): pl.pallas_call(kernel, out_shape=jax.ShapeDtypeStruct(latents.shape, BF16...  98.3 us

profile of v4, /device:TPU:1, one launch (start us, length us, event | category | flops | bytes accessed | tf_op | source)
XLA Modules:
  0.0 100.1 jit_solution(140504469044215650)
XLA Ops:
  0.0 98.3 %shard_map.64 = bf16[2,4,64,512]{3,2,1,0:T(8,128)(2,1)} custom-call(bf16[2,4,64,512]{3,2,1,0:T(8,128)(2,1)} %lat.1, bf16[27,16,512]{2,1,0:T(8,128)(2,1)} %cw.1, bf16[512,512]{1,0:T(8,128)(2,1)} %wq.1, bf16[512,512]{1,0:T(8,128)(2,1)} %wk.1, bf16[512,512]{1,0:T(8,128)(2,1)} %wv.1, bf16[512,512]{1,0:T(8,128)(2,1)} %wo.1), custom_call_target="tpu_custom_call" | custom-call | tf_op jit(solution)/shard_map/pallas_call | solution.py:453
  98.3 1.9 %copy.8 = bf16[2,4,64,512]{3,2,1,0:T(8,128)(2,1)} copy(bf16[2,4,64,512]{3,2,1,0:T(8,128)(2,1)} %shard_map.64) | data formatting | bytes 1048576

commit v5 on v4

--- a/solution.py
+++ b/solution.py
@@ -327,30 +327,33 @@
     start_1b(1)
     start_1a(2)
     start_2b(0)
-    start_2a(1)
+    start_1a(3)
     near_lines(0)
-    start_1b(2)
-    start_1a(3)
     arrived(raw.at[0:2, 5], h_recv.at[5])
     arrived(raw.at[0:2, 0], h_recv.at[6])
     arrived(raw.at[0:2, 2:4], h_recv.at[2])
     lax.fori_loop(0, 12, shift, 0)
     pending.extend((raw.at[0:2, 0], h_send.at[i]) for i in (0, 1, 3, 4, 5, 6))
     pending.append((raw.at[0:2, 0:2], h_send.at[2]))
+    start_2a(1)
+    start_1b(2)
     finish_gather(0)
+    conv(0, 0, 2)
     start_2b(1)
+    start_1a(4)
+    conv(0, 2, 5)
+    start_1b(3)
     start_2a(2)
-    start_1b(3)
-    start_1a(4)
-    conv(0, 0, 9)
+    conv(0, 5, 9)
     finish_chunk(0)
     near_lines(1)
+    finish_gather(1)
+    conv(1, 0, 2)
+    start_2b(2)
     start_1b(4)
-    finish_gather(1)
-    start_2b(2)
     start_2a(3)
     z_step(0, 1)
-    conv(1, 0, 6)
+    conv(1, 2, 6)
     near_lines(2)
     start_2a(4)
     conv(1, 6, 9)
@@ -422,13 +425,13 @@
             den[f] = total
             num[f] = part
 
+    attend([z], True)
     z_step(2, 3)
-    attend([z], True)
+    attend([zs(-1), zs(1)])
     z_step(last, 2)
-    attend([zs(-1), zs(1)])
+    attend([zs(-2), zs(2)])
     flush()
     z_step(last, 3)
-    attend([zs(-2), zs(2)])
     attend([zs(-3), zs(3)])
     for j in range(CHUNKS):
         z_step(j, 4)

time: 101 us -> 98.9 us (0.979)
  Pallas kernels: 98.3 us -> 96.7 us
    pallas_call x1, Pallas kernels: 98.3 us -> 96.7 us  [body(): pl.pallas_call(kernel, out_shape=jax.ShapeDtypeStruct(latents.shape, BF16...]
where the time goes in v5:
time: 98.9 us; the launch traced here: 98.6 us
  Pallas kernels  96.7 us (98%)
  local copies, waits for them, and re-layouts  1.87 us (2%)
    pallas_call x1, Pallas kernels, body(): pl.pallas_call(kernel, out_shape=jax.ShapeDtypeStruct(latents.shape, BF16...  96.7 us

profile of v5, /device:TPU:1, one launch (start us, length us, event | category | flops | bytes accessed | tf_op | source)
XLA Modules:
  0.0 98.6 jit_solution(99155447658773482)
XLA Ops:
  0.0 96.7 %shard_map.64 = bf16[2,4,64,512]{3,2,1,0:T(8,128)(2,1)} custom-call(bf16[2,4,64,512]{3,2,1,0:T(8,128)(2,1)} %lat.1, bf16[27,16,512]{2,1,0:T(8,128)(2,1)} %cw.1, bf16[512,512]{1,0:T(8,128)(2,1)} %wq.1, bf16[512,512]{1,0:T(8,128)(2,1)} %wk.1, bf16[512,512]{1,0:T(8,128)(2,1)} %wv.1, bf16[512,512]{1,0:T(8,128)(2,1)} %wo.1), custom_call_target="tpu_custom_call" | custom-call | tf_op jit(solution)/shard_map/pallas_call | solution.py:456
  96.7 1.9 %copy.8 = bf16[2,4,64,512]{3,2,1,0:T(8,128)(2,1)} copy(bf16[2,4,64,512]{3,2,1,0:T(8,128)(2,1)} %shard_map.64) | data formatting | bytes 1048576

commit v6 on v5

--- a/solution.py
+++ b/solution.py
@@ -355,13 +355,13 @@
     z_step(0, 1)
     conv(1, 2, 6)
     near_lines(2)
-    start_2a(4)
     conv(1, 6, 9)
     z_step(0, 2)
     finish_chunk(1)
     start_2b(3)
     finish_gather(2)
     z_step(0, 3)
+    start_2a(4)
     z_step(1, 1)
     conv(2, 0, 5)
     near_lines(3)

time: 98.9 us -> 96.8 us (0.979)
  Pallas kernels: 96.7 us -> 94.8 us
    pallas_call x1, Pallas kernels: 96.7 us -> 94.8 us  [body(): pl.pallas_call(kernel, out_shape=jax.ShapeDtypeStruct(latents.shape, BF16...]
where the time goes in v6:
time: 96.8 us; the launch traced here: 96.7 us
  Pallas kernels  94.8 us (98%)
  local copies, waits for them, and re-layouts  1.87 us (2%)
    pallas_call x1, Pallas kernels, body(): pl.pallas_call(kernel, out_shape=jax.ShapeDtypeStruct(latents.shape, BF16...  94.8 us

profile of v6, /device:TPU:1, one launch (start us, length us, event | category | flops | bytes accessed | tf_op | source)
XLA Modules:
  0.0 96.7 jit_solution(8085475834109960150)
XLA Ops:
  0.0 94.8 %shard_map.64 = bf16[2,4,64,512]{3,2,1,0:T(8,128)(2,1)} custom-call(bf16[2,4,64,512]{3,2,1,0:T(8,128)(2,1)} %lat.1, bf16[27,16,512]{2,1,0:T(8,128)(2,1)} %cw.1, bf16[512,512]{1,0:T(8,128)(2,1)} %wq.1, bf16[512,512]{1,0:T(8,128)(2,1)} %wk.1, bf16[512,512]{1,0:T(8,128)(2,1)} %wv.1, bf16[512,512]{1,0:T(8,128)(2,1)} %wo.1), custom_call_target="tpu_custom_call" | custom-call | tf_op jit(solution)/shard_map/pallas_call | solution.py:456
  94.8 1.9 %copy.8 = bf16[2,4,64,512]{3,2,1,0:T(8,128)(2,1)} copy(bf16[2,4,64,512]{3,2,1,0:T(8,128)(2,1)} %shard_map.64) | data formatting | bytes 1048576

commit v7 on v6

--- a/solution.py
+++ b/solution.py
@@ -360,10 +360,11 @@
     finish_chunk(1)
     start_2b(3)
     finish_gather(2)
+    conv(2, 0, 3)
     z_step(0, 3)
     start_2a(4)
+    conv(2, 3, 5)
     z_step(1, 1)
-    conv(2, 0, 5)
     near_lines(3)
     start_2b(4)
     conv(2, 5, 9)

time: 96.8 us -> 98 us (1.012)
  Pallas kernels: 94.8 us -> 96 us
    pallas_call x1, Pallas kernels: 94.8 us -> 96 us  [body(): pl.pallas_call(kernel, out_shape=jax.ShapeDtypeStruct(latents.shape, BF16...]
where the time goes in v7:
time: 98 us; the launch traced here: 97.9 us
  Pallas kernels  96 us (98%)
  local copies, waits for them, and re-layouts  1.87 us (2%)
    pallas_call x1, Pallas kernels, body(): pl.pallas_call(kernel, out_shape=jax.ShapeDtypeStruct(latents.shape, BF16...  96 us

profile of v7, /device:TPU:1, one launch (start us, length us, event | category | flops | bytes accessed | tf_op | source)
XLA Modules:
  0.0 97.9 jit_solution(9956943768173932123)
XLA Ops:
  0.0 96.0 %shard_map.64 = bf16[2,4,64,512]{3,2,1,0:T(8,128)(2,1)} custom-call(bf16[2,4,64,512]{3,2,1,0:T(8,128)(2,1)} %lat.1, bf16[27,16,512]{2,1,0:T(8,128)(2,1)} %cw.1, bf16[512,512]{1,0:T(8,128)(2,1)} %wq.1, bf16[512,512]{1,0:T(8,128)(2,1)} %wk.1, bf16[512,512]{1,0:T(8,128)(2,1)} %wv.1, bf16[512,512]{1,0:T(8,128)(2,1)} %wo.1), custom_call_target="tpu_custom_call" | custom-call | tf_op jit(solution)/shard_map/pallas_call | solution.py:457
  96.1 1.9 %copy.8 = bf16[2,4,64,512]{3,2,1,0:T(8,128)(2,1)} copy(bf16[2,4,64,512]{3,2,1,0:T(8,128)(2,1)} %shard_map.64) | data formatting | bytes 1048576
